TPU v7x, 256 devices: a whole 4x4x8 slice. The times are simulated.
256 devices in a mesh: dp: 32 (over y, z), expert: 8 (over x, core).
Axes of the slice: x: 4, y: 4, z: 8, core: 2. Of those that a mesh axis runs over, the one named last changes fastest.
Arguments:
- tokens: bfloat16 [4096, 4096], P('dp', 'expert'), may hold values from -24 to 24
- expert_ids: int32 [4096, 8], P('dp'), may hold values from 0 to 63, all different within a row; in each aligned block of 128 rows (0 to 127, 128 to 255, ...) at most 20 rows name the same one
- route_weights: float32 [4096, 8], P('dp'), may hold values from 0.05 to 1
- gate_weight: bfloat16 [64, 1536, 4096], P('dp', 'expert'), may hold values from -0.09375 to 0.09375
- up_weight: bfloat16 [64, 1536, 4096], P('dp', 'expert'), may hold values from -0.09375 to 0.09375
- down_weight: bfloat16 [64, 1536, 4096], P('dp', None, 'expert'), may hold values from -0.15625 to 0.15625
Outputs:
- quant_out: bfloat16 [4096, 4096], P('dp', 'expert')
- float_out: float32 [4096, 4096], P('dp', 'expert')
Inputs may be any that keep to these rules, and one draw needn't show every extreme that they name: `expert_ids`: each row names 8 different experts; every expert is named by some row; within the 128 rows of one index of dp no expert is named more than 20 times, and in every draw some expert is named exactly 20 times in some such block.
All inputs are finite; a program needn't handle non-finite values. Where the computation divides by a largest or mean magnitude, that divisor is 1e-20 or more.
Results may differ from a plain program's by a relative error of at most 0.011.
Values may be sent and summed in bfloat16 or wider, within the bound.
A program may use at most 128 MiB of HBM per device.

v0:
```python
import jax
import jax.numpy as jnp
from jax import lax
from jax.sharding import PartitionSpec as P

TOPK = 8
EXPERTS = 64
CAP = 20


TWO_PI = 6.283185307179586


def soft_level(values):
    return values - jnp.sin(TWO_PI * values) / TWO_PI


def fake_quant(values, reduce_axis, levels):
    peak_abs = jnp.max(jnp.abs(values), axis=reduce_axis, keepdims=True) + 1e-06
    return peak_abs / levels * soft_level(levels * values / peak_abs)


def slot_layout(expert_ids):
    count_rows = expert_ids.shape[0]
    flat_ids = expert_ids.reshape(-1)
    hit_mask = (flat_ids[:, None] == jnp.arange(EXPERTS, dtype=jnp.int32)[None, :]).astype(
        jnp.int32
    )
    before = jnp.cumsum(hit_mask, axis=0) - hit_mask
    slot_index = jnp.sum(before * hit_mask, axis=1)
    target = flat_ids * CAP + slot_index
    owner_token = jnp.arange(count_rows * TOPK, dtype=jnp.int32) // TOPK
    slot_table = jnp.full((EXPERTS * CAP,), -1, jnp.int32).at[target].set(owner_token)
    return (target, slot_table)


def on_device(tokens, expert_ids, route_weights, gate_weight, up_weight, down_weight):
    groups = lax.axis_size("dp")
    local_experts = gate_weight.shape[0]
    hidden_share = gate_weight.shape[1]
    target, slot_table = slot_layout(expert_ids)
    present = (slot_table >= 0)[:, None]
    source_rows = jnp.maximum(slot_table, 0)
    empty_value = jnp.zeros((), jnp.bfloat16)
    full_tokens = lax.all_gather(tokens, "expert", axis=1, tiled=True)
    outgoing = jnp.where(present, jnp.take(full_tokens, source_rows, axis=0), empty_value)
    outgoing = outgoing.reshape(groups, local_experts, CAP, full_tokens.shape[1])
    arrived = lax.all_to_all(outgoing, "dp", split_axis=0, concat_axis=2, tiled=True)
    rows = arrived[0]
    both_weight = jnp.concatenate((gate_weight, up_weight), axis=1)
    local_peak = jnp.max(jnp.abs(both_weight), axis=1).astype(jnp.float32)
    weight_peak = (
        lax.pmax(local_peak.astype(jnp.bfloat16), "expert").astype(local_peak.dtype) + 1e-06
    )
    both_float = jnp.einsum("esd,efd->esf", rows, both_weight, preferred_element_type=jnp.float32)
    hidden_float = (
        jax.nn.silu(both_float[:, :, :hidden_share]) * both_float[:, :, hidden_share:]
    ).astype(jnp.bfloat16)
    act_peak = jnp.maximum(jnp.max(jnp.abs(rows), axis=1).astype(jnp.float32), 1.0)
    smooth = jnp.sqrt(act_peak / weight_peak)
    rows_quant = fake_quant(rows.astype(jnp.float32) / smooth[:, None, :], 2, 7.0).astype(
        jnp.bfloat16
    )
    both_quant_w = fake_quant(both_weight.astype(jnp.float32) * smooth[:, None, :], 2, 7.0).astype(
        jnp.bfloat16
    )
    both_quant = jnp.einsum(
        "esd,efd->esf", rows_quant, both_quant_w, preferred_element_type=jnp.float32
    )
    hidden_quant = (
        jax.nn.silu(both_quant[:, :, :hidden_share]) * both_quant[:, :, hidden_share:]
    ).astype(jnp.bfloat16)
    wide_float, wide_quant = (
        lax.all_gather(hidden_float, "expert", axis=2, tiled=True),
        lax.all_gather(hidden_quant, "expert", axis=2, tiled=True),
    )
    out_float = jnp.einsum(
        "esf,efd->esd", wide_float, down_weight, preferred_element_type=jnp.float32
    ).astype(jnp.bfloat16)
    hidden_levels = fake_quant(wide_quant.astype(jnp.float32), 2, 7.0).astype(jnp.bfloat16)
    down_quant_w = fake_quant(down_weight.astype(jnp.float32), 1, 7.0).astype(jnp.bfloat16)
    out_quant = jnp.einsum(
        "esf,efd->esd", hidden_levels, down_quant_w, preferred_element_type=jnp.float32
    ).astype(jnp.bfloat16)
    back_quant, back_float = (
        lax.all_to_all(out_quant, "dp", split_axis=1, concat_axis=0, tiled=True),
        lax.all_to_all(out_float, "dp", split_axis=1, concat_axis=0, tiled=True),
    )
    width = back_quant.shape[-1]
    token_count = route_weights.shape[0]
    shares = route_weights / jnp.sum(route_weights, axis=1, keepdims=True)
    picked_quant = (
        jnp.take(back_quant.reshape(-1, width), target, axis=0)
        .reshape(token_count, TOPK, width)
        .astype(jnp.float32)
    )
    picked_float = (
        jnp.take(back_float.reshape(-1, width), target, axis=0)
        .reshape(token_count, TOPK, width)
        .astype(jnp.float32)
    )
    mixed_quant = jnp.sum(shares[:, :, None] * picked_quant, axis=1)
    mixed_float = jnp.sum(shares[:, :, None] * picked_float, axis=1)
    return (mixed_quant.astype(jnp.bfloat16), mixed_float)


def solution(mesh):
    in_specs = (
        P("dp", "expert"),
        P("dp", None),
        P("dp", None),
        P("dp", "expert", None),
        P("dp", "expert", None),
        P("dp", None, "expert"),
    )
    out_specs = (P("dp", "expert"), P("dp", "expert"))
    return jax.shard_map(
        on_device, mesh=mesh, in_specs=in_specs, out_specs=out_specs, check_vma=False
    )
```

profile of v0, /device:TPU:33, one launch (start us, length us, event | category | flops | bytes accessed | tf_op | source)
XLA Modules:
  0.0 768.4 jit_solution(1554965705827391001)
XLA Ops:
  7.2 0.7 all-gather.4.cloned.1.call-update
  7.9 0.8 copy.48
  8.9 18.0 %reduce-window.6 = s32[64,8,128]{2,1,0:T(8,128)S(1)} reduce-window(s32[64,8,128]{2,1,0:T(8,128)S(1)} %fusion.26, s32[]{:T(128)} %constant.48.clone.1), window={size=1x1x128 pad=0_0x0_0x127_0}, to_apply=%region_1.2 | reduce-window | flops 8323072 | bytes 524292 | tf_op jit(solution)/shard_map/reduce-window
  27.1 0.1 copy.50
  27.3 0.7 broadcast_multiply_fusion.3
  28.2 0.1 broadcast_add_fusion
  28.5 0.6 copy-done.9
  29.0 4.3 scatter_custom_fusion
  33.7 5.0 all-gather.4.cloned.1.call-done
  38.6 20.1 %gather_fusion = bf16[1280,4096]{1,0:T(8,128)(2,1)} fusion(bf16[128,4096]{1,0:T(8,128)(2,1)} %all-gather.4.cloned.1.call-done, s32[2048]{0:T(1024)S(1)} %pad_clamp_fusion), kind=kCustom, calls=%fused_computation.2 | custom fusion | bytes 20976640 | tf_op jit(solution)/shard_map/jit(_take)/gather | solution.py:46
  58.7 13.9 %gather.10 = bf16[32,2,20,4096]{3,2,1,0:T(8,128)(2,1)} reshape(bf16[1280,4096]{1,0:T(8,128)(2,1)} %gather_fusion) | data formatting | bytes 20971520 | tf_op jit(solution)/shard_map/jit(_take)/gather | solution.py:46
  72.6 6.7 select_select_fusion
  79.4 22.9 %copy.53 = bf16[32,2,20,4096]{3,1,2,0:T(2,128)(2,1)} copy(bf16[32,2,20,4096]{3,2,1,0:T(8,128)(2,1)S(1)} %select_select_fusion) | data formatting | bytes 20971520 | tf_op jit(solution)/shard_map/jit(_where)/select_n | solution.py:46
  102.3 9.8 %all-to-all-start = ((bf16[32,2,20,4096]{3,1,2,0:T(2,128)(2,1)}), bf16[32,2,20,4096]{3,1,2,0:T(2,128)(2,1)}, u32[]{:S(2)}, u32[]{:S(2)}) async-start(bf16[32,2,20,4096]{3,1,2,0:T(2,128)(2,1)} %copy.53), calls=%async_computation | async-start | bytes 20971520 | tf_op jit(solution)/shard_map/all_to_all | solution.py:48
  112.2 0.2 constant_dynamic-update-slice_fusion.1
  112.4 1.7 copy-done.5
  114.1 0.3 constant_dynamic-update-slice_fusion
  114.4 2.7 copy-done.1
  117.1 1.0 abs_reduce_fusion.3
  118.1 22.5 %pmax.7 = bf16[2,4096]{1,0:T(2,128)(2,1)S(1)} all-reduce(bf16[2,4096]{1,0:T(2,128)(2,1)S(1)} %abs_reduce_fusion.3), channel_id=1, replica_groups=mesh['dp'=32,'expert'=8] {'expert'}, use_global_device_ids=true, to_apply=%region_7.8 | all-reduce | flops 8192 | bytes 32768 | tf_op jit(solution)/shard_map/pmax | solution.py:53
  140.6 215.8 %all-to-all-done = bf16[32,2,20,4096]{3,1,2,0:T(2,128)(2,1)} async-done(((bf16[32,2,20,4096]{3,1,2,0:T(2,128)(2,1)}), bf16[32,2,20,4096]{3,1,2,0:T(2,128)(2,1)}, u32[]{:S(2)}, u32[]{:S(2)}) %all-to-all-start) | async-done | bytes 10485792 | tf_op jit(solution)/shard_map/all_to_all | solution.py:48
  356.4 16.2 %abs_reduce_fusion.2 = bf16[2,4096]{1,0:T(2,128)(2,1)S(1)} fusion(bf16[32,2,20,4096]{3,1,2,0:T(2,128)(2,1)} %all-to-all-done), kind=kLoop, calls=%fused_computation.11 | loop fusion | flops 10477568 | bytes 10502144 | tf_op jit(solution)/shard_map/reduce_max | solution.py:59
  372.7 1.7 abs_reduce_fusion.1
  374.5 19.8 %abs_reduce_fusion = f32[2,32,20]{1,2,0:T(8,128)S(1)} fusion(f32[2,4096]{1,0:T(2,128)S(1)} %fusion.27, bf16[32,2,20,4096]{3,1,2,0:T(2,128)(2,1)} %all-to-all-done), kind=kLoop, calls=%fused_computation.5 | loop fusion | flops 20970240 | bytes 10523648 | tf_op jit(solution)/shard_map/reduce_max | solution.py:19
  394.5 15.6 %copy.88 = bf16[32,2,20,4096]{3,0,2,1:T(8,128)(2,1)} copy(bf16[32,2,20,4096]{3,1,2,0:T(2,128)(2,1)} %all-to-all-done) | data formatting | bytes 20971520 | tf_op jit(solution)/shard_map/all_to_all | solution.py:48
  410.1 19.5 %copy.58 = bf16[1,2,32,20,4096]{4,1,3,2,0:T(2,128)(2,1)S(1)} copy(bf16[1,2,32,20,4096]{4,2,3,1,0:T(8,128)(2,1)} %bitcast.48) | data formatting | bytes 20971520 | tf_op jit(solution)/shard_map/all_to_all | solution.py:48
  429.6 80.6 %multiply_convert_fusion.24 = bf16[2,640,4096]{2,1,0:T(8,128)(2,1)S(1)} fusion(f32[2,640]{1,0:T(2,128)S(1)} %add.108, f32[2,4096]{1,0:T(2,128)S(1)} %fusion.27, f32[2,640]{1,0:T(2,128)S(1)} %broadcast_multiply_fusion.1, bf16[2,640,4096]{2,0,1:T(2,128)(2,1)S(1)} %bitcast.46), kind=kLoop, calls=%fused_computation.4.clone.clone.2 | loop fusion | flops 47185920 | bytes 21014528 | tf_op jit(solution)/shard_map/esd,efd->esf/dot_general | solution.py:67
  510.2 49.7 %fusion = f32[2,640,384]{1,2,0:T(8,128)S(1)} fusion(f32[2,4096]{1,0:T(2,128)S(1)} %fusion.27, bf16[2,384,4096]{2,1,0:T(8,128)(2,1)S(1)} %bitcast.50, f32[2,384]{1,0:T(2,128)S(1)} %get-tuple-element.12, f32[2,384]{1,0:T(2,128)S(1)} %get-tuple-element.11, bf16[2,640,4096]{2,1,0:T(8,128)(2,1)S(1)} %multiply_convert_fusion.24), kind=kOutput, calls=%fused_computation.12 | convolution fusion | flops 4054843392 | bytes 18782208 | tf_op jit(solution)/shard_map/esd,efd->esf/dot_general | solution.py:67
  559.9 1.1 fusion.22
  561.1 38.4 %fusion.1 = f32[2,640,384]{1,2,0:T(8,128)} fusion(bf16[2,384,4096]{2,1,0:T(8,128)(2,1)} %copy-done.1, bf16[2,640,4096]{2,0,1:T(2,128)(2,1)} %bitcast.47), kind=kOutput, calls=%fused_computation.15 | convolution fusion | flops 4026531840 | bytes 18743296 | tf_op jit(solution)/shard_map/esd,efd->esf/dot_general | solution.py:55
  599.6 2.6 fusion.21
  602.2 0.3 fusion.6
  602.5 2.5 fusion.4
  605.1 52.3 %fusion.20 = bf16[2,640,512]{2,1,0:T(8,128)(2,1)S(1)} fusion(bf16[2,1536,512]{2,1,0:T(8,128)(2,1)S(1)} %copy-done.6, f32[2,512]{1,0:T(2,128)S(1)} %get-tuple-element.10, f32[2,512]{1,0:T(2,128)S(1)} %get-tuple-element.9, bf16[2,640,1536]{1,2,0:T(8,128)(2,1)} %all-gather.6.cloned.1.call-done, f32[2,640]{1,0:T(2,128)S(1)} %get-tuple-element.8, ...), kind=kOutput, calls=%fused_computation.42 | convolution fusion | flops 2042232832 | bytes 8407040 | tf_op jit(solution)/shard_map/esf,efd->esd/dot_general | solution.py:82
  657.4 2.4 copy.61
  659.8 11.7 %all-to-all-start.1 = ((bf16[2,640,512]{2,0,1:T(2,128)(2,1)}), bf16[2,640,512]{2,0,1:T(2,128)(2,1)S(1)}, u32[]{:S(2)}, u32[]{:S(2)}) async-start(bf16[2,640,512]{2,0,1:T(2,128)(2,1)} %copy.61), calls=%async_computation.1 | async-start | bytes 2621440 | tf_op jit(solution)/shard_map/all_to_all | solution.py:86
  671.6 5.3 convolution_convert_fusion
  676.9 2.4 copy.64
  679.4 25.6 %all-to-all-done.1 = bf16[2,640,512]{2,0,1:T(2,128)(2,1)S(1)} async-done(((bf16[2,640,512]{2,0,1:T(2,128)(2,1)}), bf16[2,640,512]{2,0,1:T(2,128)(2,1)S(1)}, u32[]{:S(2)}, u32[]{:S(2)}) %all-to-all-start.1) | async-done | bytes 1310752 | tf_op jit(solution)/shard_map/all_to_all | solution.py:86
  705.0 5.9 all-to-all-start.2
  711.1 0.3 copy.62
  711.4 0.3 reshape.132
  711.7 31.0 %all-to-all-done.2 = bf16[2,640,512]{2,0,1:T(2,128)(2,1)} async-done(((bf16[2,640,512]{2,0,1:T(2,128)(2,1)}), bf16[2,640,512]{2,0,1:T(2,128)(2,1)}, u32[]{:S(2)}, u32[]{:S(2)}) %all-to-all-start.2) | async-done | bytes 1310752 | tf_op jit(solution)/shard_map/all_to_all | solution.py:87
  742.7 2.8 copy.65
  745.5 2.3 reshape.133
  747.8 5.1 gather_fusion.1
  752.9 5.1 gather_fusion.2
  757.9 3.5 fusion.18
  (63 shorter events, 1.7 us)
Async XLA Ops:
  7.2 31.5 %all-gather.4.cloned.1.call-start = ((), (), s32[]{:S(2)}) async-start(), calls=%async_computation.3 | async-start | bytes 1179648 | tf_op jit(solution)/shard_map/all_gather | solution.py:45
  8.9 49.8 %copy-start.7 = (s32[1024]{0:T(1024)}, s32[1024]{0:T(1024)S(1)}, u32[]{:S(2)}) copy-start(s32[1024]{0:T(1024)S(1)} %eq.25) | copy-start | bytes 12292
  28.4 0.6 copy-start.9
  102.3 9.9 %copy-start.4 = (bf16[2,192,4096]{2,1,0:T(8,128)(2,1)S(1)}, bf16[2,192,4096]{2,1,0:T(8,128)(2,1)}, u32[]{:S(2)}) copy-start(bf16[2,192,4096]{2,1,0:T(8,128)(2,1)} %param.11) | copy-start | bytes 9437188
  102.3 254.1 %all-to-all-start = ((bf16[32,2,20,4096]{3,1,2,0:T(2,128)(2,1)}), bf16[32,2,20,4096]{3,1,2,0:T(2,128)(2,1)}, u32[]{:S(2)}, u32[]{:S(2)}) async-start(bf16[32,2,20,4096]{3,1,2,0:T(2,128)(2,1)} %copy.53), calls=%async_computation | async-start | bytes 20971520 | tf_op jit(solution)/shard_map/all_to_all | solution.py:48
  112.1 490.4 %all-gather.6.cloned.1.call-start = ((), (), s32[]{:S(2)}) async-start(), calls=%async_computation.4 | async-start | bytes 4423680 | tf_op jit(solution)/shard_map/all_gather | solution.py:75
  112.2 1.9 copy-start.5
  114.4 2.7 copy-start.1
  356.4 16.3 %copy-start.2 = (bf16[2,384,4096]{2,1,0:T(8,128)(2,1)S(1)}, bf16[2,384,4096]{2,1,0:T(8,128)(2,1)}, u32[]{:S(2)}) copy-start(bf16[2,384,4096]{2,1,0:T(8,128)(2,1)} %copy-done.1) | copy-start | bytes 18874372
  410.1 100.1 %slice-start = ((s8[6291456]{0:T(1024)(128)(4,1)}), s8[4194304]{0:T(1024)(128)(4,1)S(1)}, s32[]{:S(2)}) async-start(s8[6291456]{0:T(1024)(128)(4,1)} %bitcast.49), calls=%async_computation.6 | async-start | bytes 8388608
  429.6 80.6 %copy-start = (bf16[1,2,32,20,4096]{4,1,3,2,0:T(2,128)(2,1)}, bf16[1,2,32,20,4096]{4,1,3,2,0:T(2,128)(2,1)S(1)}, u32[]{:S(2)}) copy-start(bf16[1,2,32,20,4096]{4,1,3,2,0:T(2,128)(2,1)S(1)} %copy.58) | copy-start | bytes 31457284
  429.6 80.6 %slice-start.1 = ((s8[6291456]{0:T(1024)(128)(4,1)}), s8[2097152]{0:T(1024)(128)(4,1)S(1)}, s32[]{:S(2)}) async-start(s8[6291456]{0:T(1024)(128)(4,1)} %bitcast.49), calls=%async_computation.7 | async-start | bytes 4194304
  561.1 41.1 %copy-start.6 = (bf16[2,1536,512]{2,1,0:T(8,128)(2,1)S(1)}, bf16[2,1536,512]{2,1,0:T(8,128)(2,1)}, u32[]{:S(2)}) copy-start(bf16[2,1536,512]{2,1,0:T(8,128)(2,1)} %param.13) | copy-start | bytes 9437188
  561.1 110.5 %all-gather.8.cloned.1.call-start = ((), (), s32[]{:S(2)}) async-start(), calls=%async_computation.5 | async-start | bytes 4423680 | tf_op jit(solution)/shard_map/all_gather | solution.py:74
  659.8 45.1 %all-to-all-start.1 = ((bf16[2,640,512]{2,0,1:T(2,128)(2,1)}), bf16[2,640,512]{2,0,1:T(2,128)(2,1)S(1)}, u32[]{:S(2)}, u32[]{:S(2)}) async-start(bf16[2,640,512]{2,0,1:T(2,128)(2,1)} %copy.61), calls=%async_computation.1 | async-start | bytes 2621440 | tf_op jit(solution)/shard_map/all_to_all | solution.py:86
  671.6 39.3 %copy-start.11 = (f32[128,8]{0,1:T(8,128)S(1)}, f32[128,8]{0,1:T(8,128)}, u32[]{:S(2)}) copy-start(f32[128,8]{0,1:T(8,128)} %param.10) | copy-start | bytes 12292
  671.6 39.4 %copy-start.8 = (s32[1024]{0:T(1024)S(1)}, s32[1024]{0:T(1024)}, u32[]{:S(2)}) copy-start(s32[1024]{0:T(1024)} %copy-done.7) | copy-start | bytes 12292
  671.6 39.4 %copy-start.10 = (s32[1024]{0:T(1024)S(1)}, s32[1024]{0:T(1024)}, u32[]{:S(2)}) copy-start(s32[1024]{0:T(1024)} %copy-done.9) | copy-start | bytes 12292
  705.0 37.8 %all-to-all-start.2 = ((bf16[2,640,512]{2,0,1:T(2,128)(2,1)}), bf16[2,640,512]{2,0,1:T(2,128)(2,1)}, u32[]{:S(2)}, u32[]{:S(2)}) async-start(bf16[2,640,512]{2,0,1:T(2,128)(2,1)} %copy.64), calls=%async_computation.2 | async-start | bytes 2621440 | tf_op jit(solution)/shard_map/all_to_all | solution.py:87
  752.9 5.1 copy-start.3
Sparse Core Ops, SparseCore 0:
  9.8 28.7 all-gather.3
  561.2 36.5 all-gather.5
  602.3 36.5 all-gather.7
where the time goes:
time: 779 us; the launch traced here: 768 us
  waiting for transfers between devices  278 us (36%)
  other arithmetic  155 us (20%)
  matrix products  146 us (19%)
  local copies, waits for them, and re-layouts  125 us (16%)
  starting transfers between devices  27.6 us (4%)
  blocking collectives  22.5 us (3%)
  between operations  14.7 us (2%)
    all_to_all x1, waiting for transfers between devices, on_device(): lax.all_to_all(outgoing, 'dp', split_axis=0, concat_axis=2, tiled=True)  216 us
    dot_general x1, other arithmetic, on_device(): jnp.einsum('esd,efd->esf', rows_quant, both_quant_w, preferred_element_ty...  80.6 us
    dot_general x1, matrix products, on_device(): jnp.einsum('esf,efd->esd', hidden_levels, down_quant_w, preferred_element...  52.3 us
    dot_general x1, matrix products, on_device(): jnp.einsum('esd,efd->esf', rows_quant, both_quant_w, preferred_element_ty...  49.7 us
    dot_general x1, matrix products, on_device(): jnp.einsum('esd,efd->esf', rows, both_weight, preferred_element_type=jnp....  38.4 us
    all_to_all x2, local copies, waits for them, and re-layouts, on_device(): lax.all_to_all(outgoing, 'dp', split_axis=0, concat_axis=2, tiled=True)  35.1 us
    gather x2, local copies, waits for them, and re-layouts, on_device(): jnp.take(full_tokens, source_rows, axis=0)  34 us
    all_to_all x1, waiting for transfers between devices, on_device(): lax.all_to_all(out_float, 'dp', split_axis=1, concat_axis=0, tiled=True)  31 us
  transfers between devices with their start and end apart: 6, of which 4 were waited for; matrix products, arithmetic and copies ran while one was open for 17% of the time, Pallas kernels for 0%

commit v1 on v0

v1 whole, which is shorter than its diff:
```python
import functools

import jax
import jax.numpy as jnp
from jax import lax
from jax.experimental import pallas as pl
from jax.experimental.pallas import tpu as pltpu
from jax.sharding import PartitionSpec as P

MESH = pl.DeviceIdType.MESH
CAP = 20
HEAD = 16
REST = CAP - HEAD
BF = jnp.bfloat16
F32 = jnp.float32
COEF = (6.579714691987998, -12.986868688853527, 12.19161471791364, -6.570950351250938, 1.9706418898295621)
ROUND = 12582912.0


def soft_level(values):
    whole = (values + ROUND) - ROUND
    rest = values - whole
    square = rest * rest
    poly = COEF[4]
    for coef in COEF[3::-1]:
        poly = poly * square + coef
    return whole + (rest * square) * poly


def dot_nt(a, b):
    return lax.dot_general(a, b, (((1,), (1,)), ((), ())), preferred_element_type=F32)


def dot_nn(a, b):
    return lax.dot_general(a, b, (((1,), (0,)), ((), ())), preferred_element_type=F32)


def iota(shape, axis):
    return lax.broadcasted_iota(jnp.int32, shape, axis)


def layer_kernel(
    groups,
    ring,
    tok_ref,
    ids_t_ref,
    ids_ref,
    route_ref,
    gate_hbm,
    up_hbm,
    down_hbm,
    quant_ref,
    float_ref,
    tok,
    send_head,
    send_rest,
    rows,
    rest_in,
    weight,
    weight_q,
    down,
    down_q,
    rows_q,
    acc_float,
    acc_quant,
    hid_float,
    hid_quant,
    hid_level,
    peak_own,
    peak_in,
    smooth,
    inv_smooth,
    row_peak,
    row_mul,
    row_div,
    col_mul,
    col_div,
    mix_head,
    mix_rest,
    outf_head,
    outf_rest,
    outq_head,
    outq_rest,
    rest_acc,
    backf_head,
    backf_rest,
    backq_head,
    backq_rest,
    part,
    part_in,
    load_sem,
    swap_send,
    swap_recv,
    a2a_send,
    a2a_recv,
    small_send,
    small_recv,
    ring_send,
    ring_recv,
    ex_send,
    ex_recv,
):
    me = lax.axis_index("dp")
    seat = lax.axis_index("expert")
    x = seat // 2
    core = seat % 2
    width = tok_ref.shape[1]
    wide = 2 * width
    quarter = wide // 4
    hid = gate_hbm.shape[1]
    hid2 = 2 * hid
    count = groups * CAP
    half = count // 2
    n_head = groups * HEAD
    n_rest = groups * REST
    top = ids_ref.shape[1]
    toks = tok_ref.shape[0]
    lanes = min(512, wide)
    block = 128 if count % 128 == 0 else count
    n_block = count // block
    hidden_all = ring * hid2

    partner = (me, x * 2 + 1 - core)

    def along(k):
        return (me, lax.rem(x + k, ring) * 2 + core)

    def peer(k):
        return (lax.rem(me + k, groups), seat)

    loads = []
    for s in range(ring):
        for g, src in enumerate((gate_hbm, up_hbm)):
            loads.append(
                pltpu.make_async_copy(
                    src.at[core, :, pl.ds(s * wide, wide)],
                    weight.at[s, pl.ds(pl.multiple_of(g * hid2 + core * hid, 8), hid), :],
                    load_sem.at[2 * s + g],
                )
            )
    loads.append(
        pltpu.make_async_copy(
            down_hbm.at[core],
            down.at[:, pl.ds(pl.multiple_of(core * width, 128), width)],
            load_sem.at[2 * ring],
        )
    )
    loads[-1].start()
    for copy in loads[:-1]:
        copy.start()

    barrier = pltpu.get_barrier_semaphore()
    pl.semaphore_signal(barrier, inc=1, device_id=partner, device_id_type=MESH)
    for k in range(1, ring):
        pl.semaphore_signal(barrier, inc=1, device_id=along(k), device_id_type=MESH)

    def greet(k, carry):
        pl.semaphore_signal(barrier, inc=1, device_id=peer(k), device_id_type=MESH)
        return carry

    lax.fori_loop(1, groups, greet, 0)

    before = (iota((toks, toks), 0) < iota((toks, toks), 1)).astype(BF)
    row_id = iota((n_head, toks), 0)
    hit = jnp.zeros((n_head, toks), F32)
    wanted = (row_id // HEAD) * 2 + core
    for k in range(top):
        hit = hit + (ids_t_ref[k : k + 1, :] == wanted).astype(F32)
    slot = dot_nn(hit.astype(BF), before)
    pick_head = jnp.where(slot == (row_id % HEAD).astype(F32), hit, 0.0).astype(BF)
    pick_rest = jnp.where(slot == (HEAD + row_id % REST).astype(F32), hit, 0.0)
    part_id = (row_id // REST) % 4

    pl.semaphore_wait(barrier, 1 + (ring - 1) + (groups - 1))

    own_cols = pl.ds(pl.multiple_of(core * width, 128), width)
    tok_copy = pltpu.make_async_remote_copy(
        src_ref=tok_ref,
        dst_ref=tok.at[:, own_cols],
        send_sem=swap_send.at[0],
        recv_sem=swap_recv.at[0],
        device_id=partner,
        device_id_type=MESH,
    )
    tok_copy.start()
    tok[:, own_cols] = tok_ref[...]
    swaps = [
        pltpu.make_async_remote_copy(
            src_ref=down_hbm.at[1 - core],
            dst_ref=down.at[:, own_cols],
            send_sem=swap_send.at[1],
            recv_sem=swap_recv.at[1],
            device_id=partner,
            device_id_type=MESH,
        )
    ]
    for s in range(ring):
        for g, src in enumerate((gate_hbm, up_hbm)):
            swaps.append(
                pltpu.make_async_remote_copy(
                    src_ref=src.at[1 - core, :, pl.ds(s * wide, wide)],
                    dst_ref=weight.at[s, pl.ds(pl.multiple_of(g * hid2 + core * hid, 8), hid), :],
                    send_sem=swap_send.at[2 + 2 * s + g],
                    recv_sem=swap_recv.at[2 + 2 * s + g],
                    device_id=partner,
                    device_id_type=MESH,
                )
            )
    tok_copy.wait()
    for copy in swaps:
        copy.start()

    send_head[...] = dot_nn(pick_head, tok[...]).astype(BF)
    chosen = jnp.zeros((n_head, quarter), F32)
    for q in range(4):
        chosen = chosen + dot_nn(
            jnp.where(part_id == q, pick_rest, 0.0).astype(BF), tok[:, q * quarter : (q + 1) * quarter]
        )
    send_rest[...] = chosen.astype(BF)

    my_head = pl.ds(pl.multiple_of(me * HEAD, HEAD), HEAD)

    def exchange(number, src_head, src_rest, dst_head, dst_rest):
        def copies(k):
            to = pl.ds(pl.multiple_of(lax.rem(me + k, groups) * HEAD, HEAD), HEAD)
            return (
                pltpu.make_async_remote_copy(
                    src_ref=src_head.at[to, :],
                    dst_ref=dst_head.at[my_head, :],
                    send_sem=a2a_send.at[number, 0],
                    recv_sem=a2a_recv.at[number, 0],
                    device_id=peer(k),
                    device_id_type=MESH,
                ),
                pltpu.make_async_remote_copy(
                    src_ref=src_rest.at[to, :],
                    dst_ref=dst_rest.at[my_head, :],
                    send_sem=a2a_send.at[number, 1],
                    recv_sem=a2a_recv.at[number, 1],
                    device_id=peer(k),
                    device_id_type=MESH,
                ),
            )

        def begin(k, carry):
            for copy in copies(k):
                copy.start()
            return carry

        lax.fori_loop(1, groups, begin, 0)
        dst_head[my_head, :] = src_head[my_head, :]
        dst_rest[my_head, :] = src_rest[my_head, :]

        total = pl.ds(0, (groups - 1) * HEAD)

        def waiting(index, src, dst):
            return pltpu.make_async_remote_copy(
                src_ref=src.at[total, :],
                dst_ref=dst.at[total, :],
                send_sem=a2a_send.at[number, index],
                recv_sem=a2a_recv.at[number, index],
                device_id=peer(1),
                device_id_type=MESH,
            )

        return (waiting(0, src_head, dst_head), waiting(1, src_rest, dst_rest))

    slab = rows.at[x]
    sent = exchange(0, send_head, send_rest, slab, rest_in)

    ratio = route_ref[...]
    ratio = ratio / jnp.sum(ratio, axis=1, keepdims=True)
    lane_id = iota((toks, n_head), 1)
    wanted_t = (lane_id // HEAD) * 2 + core
    hit_t = jnp.zeros((toks, n_head), F32)
    share_t = jnp.zeros((toks, n_head), F32)
    for k in range(top):
        same = ids_ref[:, k : k + 1] == wanted_t
        hit_t = hit_t + same.astype(F32)
        share_t = share_t + jnp.where(same, ratio[:, k : k + 1], 0.0)
    before_t = (iota((toks, toks), 1) < iota((toks, toks), 0)).astype(BF)
    slot_t = dot_nn(before_t, hit_t.astype(BF))
    for which, ref in (
        ((lane_id % HEAD).astype(F32), mix_head),
        ((HEAD + lane_id % REST).astype(F32), mix_rest),
    ):
        value = jnp.where(slot_t == which, share_t, 0.0)
        high = value.astype(BF)
        ref[0:toks, :] = high
        ref[toks:, :] = (value - high.astype(F32)).astype(BF)

    loads[-1].wait()
    swaps[0].wait()
    for n in range(wide // lanes):
        cols = slice(n * lanes, (n + 1) * lanes)

        def down_peak(i, best):
            at = pl.ds(pl.multiple_of(i * 16, 16), 16)
            return jnp.maximum(best, jnp.abs(down[at, cols].astype(F32)))

        best = lax.fori_loop(0, hidden_all // 16, down_peak, jnp.zeros((16, lanes), F32))
        peak = jnp.max(best, axis=0, keepdims=True) + 1e-06
        col_mul[:, cols] = jnp.broadcast_to(7.0 / peak, (8, lanes))
        col_div[:, cols] = jnp.broadcast_to(peak / 7.0, (8, lanes))

        def down_level(i, carry):
            at = pl.ds(pl.multiple_of(i * 16, 16), 16)
            value = down[at, cols].astype(F32)
            mul = jnp.concatenate((col_mul[:, cols], col_mul[:, cols]), axis=0)
            div = jnp.concatenate((col_div[:, cols], col_div[:, cols]), axis=0)
            down_q[at, cols] = (div * soft_level(value * mul)).astype(BF)
            return carry

        lax.fori_loop(0, hidden_all // 16, down_level, 0)

    for s in range(ring):
        loads[2 * s].wait()
        loads[2 * s + 1].wait()
        swaps[1 + 2 * s].wait()
        swaps[2 + 2 * s].wait()
        for n in range(wide // lanes):
            cols = slice(n * lanes, (n + 1) * lanes)

            def weight_top(i, best):
                at = pl.ds(pl.multiple_of(i * 16, 16), 16)
                return jnp.maximum(best, jnp.abs(weight[s, at, cols].astype(F32)))

            best = lax.fori_loop(0, 2 * hid2 // 16, weight_top, jnp.zeros((16, lanes), F32))
            peak_own[s, :, cols] = jnp.broadcast_to(jnp.max(best, axis=0, keepdims=True), (8, lanes))

    def small(number, k, src, dst):
        return pltpu.make_async_remote_copy(
            src_ref=src,
            dst_ref=dst,
            send_sem=small_send.at[number, k - 1],
            recv_sem=small_recv.at[number, k - 1],
            device_id=along(k),
            device_id_type=MESH,
        )

    peak_copies = [
        small(0, k, peak_own.at[lax.rem(x + k, ring)], peak_in.at[k - 1]) for k in range(1, ring)
    ]
    for copy in peak_copies:
        copy.start()
    for copy in peak_copies:
        copy.wait()
    weight_peak = peak_own[x]
    for k in range(1, ring):
        weight_peak = jnp.maximum(weight_peak, peak_in[k - 1])

    for copy in sent:
        copy.wait_send()
        copy.wait_recv()
    spread = iota((n_rest, n_head), 1)
    home = iota((n_rest, n_head), 0)
    same_row = (spread // HEAD == home // REST) & (spread % REST == home % REST)
    for q in range(4):
        order = (same_row & ((spread // REST) % 4 == q)).astype(F32).astype(BF)
        slab[n_head:, q * quarter : (q + 1) * quarter] = dot_nn(order, rest_in[...]).astype(BF)

    for n in range(wide // lanes):
        cols = slice(n * lanes, (n + 1) * lanes)

        def act_top(i, best):
            at = pl.ds(pl.multiple_of(i * 16, 16), 16)
            return jnp.maximum(best, jnp.abs(rows[x, at, cols].astype(F32)))

        best = lax.fori_loop(0, count // 16, act_top, jnp.zeros((16, lanes), F32)) if count % 16 == 0 else jnp.abs(
            rows[x, :, cols].astype(F32)
        )
        act_peak = jnp.maximum(jnp.max(best, axis=0, keepdims=True), 1.0)
        value = jnp.sqrt(act_peak / (weight_peak[:, cols] + 1e-06))
        smooth[x, :, cols] = value
        inv_smooth[x, :, cols] = 1.0 / value
    smooth_copies = [small(1, k, smooth.at[x], smooth.at[x]) for k in range(1, ring)]
    for copy in smooth_copies:
        copy.start()

    eye = iota((block, block), 0) == iota((block, block), 1)
    top_rows = []
    for b in range(n_block):
        best = jnp.zeros((block, 128 if wide >= 128 else wide), F32)
        step = best.shape[1]
        for n in range(wide // step):
            cols = slice(n * step, (n + 1) * step)
            value = rows[x, b * block : (b + 1) * block, cols].astype(F32) * inv_smooth[x, 0:1, cols]
            best = jnp.maximum(best, jnp.abs(value))
        tall = jnp.max(best, axis=1, keepdims=True)
        top_rows.append(jnp.sum(jnp.where(eye, tall, 0.0), axis=0, keepdims=True))
    row_peak[x] = jnp.zeros((8, block), F32)
    for b in range(n_block):
        row_peak[x, b : b + 1, :] = top_rows[b]
    peak_rows = [small(2, k, row_peak.at[x], row_peak.at[x]) for k in range(1, ring)]
    for copy in peak_rows:
        copy.start()

    def hop(number, ref, way, step):
        mag = step // 2
        if way == 0:
            owner = lax.rem(x - mag + ring, ring)
            part_of = step % 2
            to = along(1)
        else:
            owner = lax.rem(x + mag, ring)
            part_of = 1 - step % 2
            to = along(ring - 1)
        at = pl.ds(part_of * half, half)
        return pltpu.make_async_remote_copy(
            src_ref=ref.at[owner, at, :],
            dst_ref=ref.at[owner, at, :],
            send_sem=ring_send.at[number, way, step],
            recv_sem=ring_recv.at[number, way, step],
            device_id=to,
            device_id_type=MESH,
        )

    def landed(number, ref, way, step):
        mag = 1 + step // 2
        if way == 0:
            owner = lax.rem(x - mag + ring, ring)
            part_of = step % 2
        else:
            owner = lax.rem(x + mag, ring)
            part_of = 1 - step % 2
        at = pl.ds(part_of * half, half)
        copy = pltpu.make_async_remote_copy(
            src_ref=ref.at[owner, at, :],
            dst_ref=ref.at[owner, at, :],
            send_sem=ring_send.at[number, way, step],
            recv_sem=ring_recv.at[number, way, step],
            device_id=along(1),
            device_id_type=MESH,
        )
        return copy, owner, part_of

    def launch(number, ref):
        for step in range(2):
            for way in range(2):
                hop(number, ref, way, step).start()

    launch(0, rows)

    for copy in smooth_copies:
        copy.wait()

    def weight_level(i, carry):
        at = pl.ds(pl.multiple_of(i * 16, 16), 16)
        best = jnp.zeros((16, lanes), F32)
        for s in range(ring):
            for n in range(wide // lanes):
                cols = slice(n * lanes, (n + 1) * lanes)
                best = jnp.maximum(best, jnp.abs(weight[s, at, cols].astype(F32) * smooth[s, 0:1, cols]))
        peak = jnp.max(best, axis=1, keepdims=True) + 1e-06
        mul = 7.0 / peak
        div = peak / 7.0
        for s in range(ring):
            for n in range(wide // lanes):
                cols = slice(n * lanes, (n + 1) * lanes)
                value = weight[s, at, cols].astype(F32) * smooth[s, 0:1, cols]
                weight_q[s, at, cols] = (div * soft_level(value * mul)).astype(BF)
        return carry

    lax.fori_loop(0, 2 * hid2 // 16, weight_level, 0)

    for copy in peak_rows:
        copy.wait()
    best_row = row_peak[0]
    for s in range(1, ring):
        best_row = jnp.maximum(best_row, row_peak[s])
    for s in range(ring):
        inv_smooth[s, :, :] = 1.0 / smooth[s]
    for b in range(n_block):
        flat = jnp.broadcast_to(best_row[b : b + 1, :], (block, block))
        tall = jnp.sum(jnp.where(eye, flat, 0.0), axis=1, keepdims=True) + 1e-06
        row_mul[b * block : (b + 1) * block, :] = jnp.broadcast_to(7.0 / tall, (block, 128))
        row_div[b * block : (b + 1) * block, :] = jnp.broadcast_to(tall / 7.0, (block, 128))

    acc_float[...] = jnp.zeros_like(acc_float)
    acc_quant[...] = jnp.zeros_like(acc_quant)

    strip = 16 if half % 16 == 0 else half

    def use(owner, part_of):
        at = pl.ds(part_of * half, half)
        acc_float[at, :] += dot_nt(rows[owner, at, :], weight[owner])

        def row_level(i, carry):
            here = pl.ds(part_of * half + i * strip, strip)
            out = pl.ds(i * strip, strip)
            mul = row_mul[here, 0:1]
            div = row_div[here, 0:1]
            for n in range(wide // lanes):
                cols = slice(n * lanes, (n + 1) * lanes)
                value = rows[owner, here, cols].astype(F32) * inv_smooth[owner, 0:1, cols]
                rows_q[out, cols] = (div * soft_level(value * mul)).astype(BF)
            return carry

        lax.fori_loop(0, half // strip, row_level, 0)
        acc_quant[at, :] += dot_nt(rows_q[...], weight_q[owner])

    def own_half(i, carry):
        use(x, i)
        return carry

    lax.fori_loop(0, 2, own_half, 0)

    def arrival(step, carry):
        for way in range(2):
            copy, owner, part_of = landed(0, rows, way, step)
            copy.wait_recv()

            @pl.when(step == 0)
            def _():
                hop(0, rows, way, 2).start()

            use(owner, part_of)
        return carry

    lax.fori_loop(0, 3, arrival, 0)

    def activate(acc, out):
        def piece(i, carry):
            at = pl.ds(pl.multiple_of(i * strip, strip), strip)
            gate = acc[at, 0:hid2]
            out[x, at, :] = (gate / (1.0 + jnp.exp(-gate)) * acc[at, hid2:]).astype(BF)
            return carry

        lax.fori_loop(0, count // strip, piece, 0)

    def relay(number, ref):
        for way in range(2):
            landed(number, ref, way, 0)[0].wait_recv()
            hop(number, ref, way, 2).start()

    def finish(number, ref):
        for step in range(1, 3):
            for way in range(2):
                landed(number, ref, way, step)[0].wait_recv()

    def drain(number, ref):
        for step in range(3):
            for way in range(2):
                hop(number, ref, way, step).wait_send()

    turn = iota((n_head, n_rest), 0)
    base = iota((n_head, n_rest), 1)
    back_row = (turn // HEAD == base // REST) & (turn % REST == base % REST)
    turn_part = (turn // REST) % 4

    def project(hidden, matrix, head, rest):
        rest_acc[...] = jnp.zeros_like(rest_acc)

        def piece(q, carry):
            cols = pl.ds(pl.multiple_of(q * quarter, quarter), quarter)
            total = dot_nn(hidden[0], matrix[0:hid2, cols])
            for s in range(1, ring):
                total = total + dot_nn(hidden[s], matrix[s * hid2 : (s + 1) * hid2, cols])
            total = total.astype(BF)
            head[:, cols] = total[:n_head]
            order = (back_row & (turn_part == q)).astype(F32).astype(BF)
            rest_acc[...] += dot_nn(order, total[n_head:])
            return carry

        lax.fori_loop(0, 4, piece, 0)
        rest[...] = rest_acc[...].astype(BF)

    activate(acc_float, hid_float)
    launch(1, hid_float)
    activate(acc_quant, hid_quant)
    relay(1, hid_float)
    launch(2, hid_quant)
    finish(1, hid_float)
    project(hid_float, down, outf_head, outf_rest)
    sent_float = exchange(1, outf_head, outf_rest, backf_head, backf_rest)
    relay(2, hid_quant)
    finish(2, hid_quant)

    def level(i, carry):
        at = pl.ds(pl.multiple_of(i * strip, strip), strip)
        best = jnp.zeros((strip, hid2), F32)
        for s in range(ring):
            best = jnp.maximum(best, jnp.abs(hid_quant[s, at, :].astype(F32)))
        peak = jnp.max(best, axis=1, keepdims=True) + 1e-06
        mul = 7.0 / peak
        div = peak / 7.0
        for s in range(ring):
            value = hid_quant[s, at, :].astype(F32)
            hid_level[s, at, :] = (div * soft_level(value * mul)).astype(BF)
        return carry

    lax.fori_loop(0, count // strip, level, 0)
    project(hid_level, down_q, outq_head, outq_rest)
    sent_quant = exchange(2, outq_head, outq_rest, backq_head, backq_rest)

    def combine(number, head, rest):
        mixed = dot_nn(mix_head[...], head[...])
        mixed = mixed[:toks] + mixed[toks:]
        quarter_of = (iota((2 * toks, n_head), 1) // REST) % 4
        for q in range(4):
            weights = jnp.where(quarter_of == q, mix_rest[...].astype(F32), 0.0).astype(BF)
            extra = dot_nn(weights, rest[...])
            cols = slice(q * quarter, (q + 1) * quarter)
            first = (q * quarter) // width
            inner = q * quarter - first * width
            part[number, first, :, inner : inner + quarter] = mixed[:, cols] + extra[:toks] + extra[toks:]
        copy = pltpu.make_async_remote_copy(
            src_ref=part.at[number, 1 - core],
            dst_ref=part_in.at[number],
            send_sem=ex_send.at[number],
            recv_sem=ex_recv.at[number],
            device_id=partner,
            device_id_type=MESH,
        )
        copy.start()
        return copy

    for copy in sent_float:
        copy.wait_recv()
    half_float = combine(0, backf_head, backf_rest)
    half_float.wait()
    float_ref[...] = part[0, core] + part_in[0]
    for copy in sent_quant:
        copy.wait_recv()
    half_quant = combine(1, backq_head, backq_rest)

    for copy in sent_float:
        copy.wait_send()
    for copy in sent_quant:
        copy.wait_send()
    for number, ref in enumerate((rows, hid_float, hid_quant)):
        drain(number, ref)
    half_quant.wait()
    quant_ref[...] = (part[1, core] + part_in[1]).astype(BF)


def solution(mesh):
    groups = mesh.shape["dp"]
    ring = mesh.shape["expert"] // 2

    def on_device(tokens, expert_ids, route_weights, gate_weight, up_weight, down_weight):
        toks, width = tokens.shape
        wide = 2 * width
        quarter = wide // 4
        hid = gate_weight.shape[1]
        hid2 = 2 * hid
        count = groups * CAP
        half = count // 2
        n_head = groups * HEAD
        hidden_all = ring * hid2
        block = 128 if count % 128 == 0 else count
        vmem = pltpu.VMEM
        dma = pltpu.SemaphoreType.DMA
        here = pl.BlockSpec(memory_space=pltpu.VMEM)
        away = pl.BlockSpec(memory_space=pl.ANY)
        return pl.pallas_call(
            functools.partial(layer_kernel, groups, ring),
            name="moe_layer",
            out_shape=(
                jax.ShapeDtypeStruct((toks, width), BF),
                jax.ShapeDtypeStruct((toks, width), F32),
            ),
            in_specs=[here, here, here, here, away, away, away],
            out_specs=(here, here),
            scratch_shapes=[
                vmem((toks, wide), BF),
                vmem((n_head, wide), BF),
                vmem((n_head, quarter), BF),
                vmem((ring, count, wide), BF),
                vmem((n_head, quarter), BF),
                vmem((ring, 2 * hid2, wide), BF),
                vmem((ring, 2 * hid2, wide), BF),
                vmem((hidden_all, wide), BF),
                vmem((hidden_all, wide), BF),
                vmem((half, wide), BF),
                vmem((count, 2 * hid2), F32),
                vmem((count, 2 * hid2), F32),
                vmem((ring, count, hid2), BF),
                vmem((ring, count, hid2), BF),
                vmem((ring, count, hid2), BF),
                vmem((ring, 8, wide), F32),
                vmem((ring - 1, 8, wide), F32),
                vmem((ring, 8, wide), F32),
                vmem((ring, 8, wide), F32),
                vmem((ring, 8, block), F32),
                vmem((count, 128), F32),
                vmem((count, 128), F32),
                vmem((8, wide), F32),
                vmem((8, wide), F32),
                vmem((2 * toks, n_head), BF),
                vmem((2 * toks, n_head), BF),
                vmem((n_head, wide), BF),
                vmem((n_head, quarter), BF),
                vmem((n_head, wide), BF),
                vmem((n_head, quarter), BF),
                vmem((n_head, quarter), F32),
                vmem((n_head, wide), BF),
                vmem((n_head, quarter), BF),
                vmem((n_head, wide), BF),
                vmem((n_head, quarter), BF),
                vmem((2, 2, toks, width), F32),
                vmem((2, toks, width), F32),
                dma((2 * ring + 1,)),
                dma((2 + 2 * ring,)),
                dma((2 + 2 * ring,)),
                dma((3, 2)),
                dma((3, 2)),
                dma((3, ring - 1)),
                dma((3, ring - 1)),
                dma((3, 2, 3)),
                dma((3, 2, 3)),
                dma((2,)),
                dma((2,)),
            ],
            compiler_params=pltpu.CompilerParams(
                collective_id=0, has_side_effects=True, vmem_limit_bytes=64 * 1024 * 1024 - 128 * 1024
            ),
        )(
            tokens,
            expert_ids.T,
            expert_ids,
            route_weights,
            gate_weight,
            up_weight,
            down_weight,
        )

    in_specs = (
        P("dp", "expert"),
        P("dp", None),
        P("dp", None),
        P("dp", "expert", None),
        P("dp", "expert", None),
        P("dp", None, "expert"),
    )
    out_specs = (P("dp", "expert"), P("dp", "expert"))
    return jax.shard_map(
        on_device, mesh=mesh, in_specs=in_specs, out_specs=out_specs, check_vma=False
    )
```

time: 779 us -> 192 us (0.25)
  waiting for transfers between devices: 278 us -> 0 us
  Pallas kernels: 0 us -> 182 us
  other arithmetic: 155 us -> 0 us
  matrix products: 146 us -> 0 us
  local copies, waits for them, and re-layouts: 125 us -> 6.07 us
  starting transfers between devices: 27.6 us -> 0 us
  blocking collectives: 22.5 us -> 0 us
  between operations: 14.7 us -> 0.64 us
    all_to_all x3 -> x0, waiting for transfers between devices: 272 us -> none  [the longest x1 216 us: on_device(): lax.all_to_all(outgoing, 'dp', split_axis=0, concat_axis=2, tiled=True)]
    pallas_call x0 -> x1, Pallas kernels: none -> 182 us  [on_device(): pl.pallas_call(functools.partial(layer_kernel, groups, ring), name='moe_l...]
    dot_general x4 -> x0, matrix products: 146 us -> none  [the longest x1 52.3 us: on_device(): jnp.einsum('esf,efd->esd', hidden_levels, down_quant_w, preferred_element...]
    dot_general x1 -> x0, other arithmetic: 80.6 us -> none  [on_device(): jnp.einsum('esd,efd->esf', rows_quant, both_quant_w, preferred_element_ty...]
    gather x4 -> x0, local copies, waits for them, and re-layouts: 44.1 us -> none  [the longest x2 34 us: on_device(): jnp.take(full_tokens, source_rows, axis=0)]
    reduce_max x6 -> x0, other arithmetic: 41.6 us -> none  [the longest x4 24.3 us: fake_quant(): peak_abs = jnp.max(jnp.abs(values), axis=reduce_axis, keepdims=True) + 1e-06]
    all_to_all x4 -> x0, local copies, waits for them, and re-layouts: 38.2 us -> none  [the longest x2 35.1 us: on_device(): lax.all_to_all(outgoing, 'dp', split_axis=0, concat_axis=2, tiled=True)]
    all_to_all x3 -> x0, starting transfers between devices: 27.4 us -> none  [the longest x1 11.7 us: on_device(): lax.all_to_all(out_quant, 'dp', split_axis=1, concat_axis=0, tiled=True)]
  transfers between devices with their start and end apart: 6 -> 0, of which waited for: 4 -> 0; matrix products, arithmetic and copies ran while one was open for 17% -> 0% of each run, Pallas kernels for 0% -> 0%
where the time goes in v1:
time: 192 us; the launch traced here: 188 us
  Pallas kernels  182 us (95%)
  local copies, waits for them, and re-layouts  6.07 us (3%)
    pallas_call x1, Pallas kernels, on_device(): pl.pallas_call(functools.partial(layer_kernel, groups, ring), name='moe_l...  182 us
    unnamed x4, local copies, waits for them, and re-layouts  6.07 us

profile of v1, /device:TPU:33, one launch (start us, length us, event | category | flops | bytes accessed | tf_op | source)
XLA Modules:
  0.0 188.3 jit_solution(9443224078348943653)
XLA Ops:
  0.6 1.4 copy.9.route_ref
  2.0 1.4 copy.8.ids_ref
  3.5 181.6 %moe_layer.1 = (bf16[128,512]{1,0:T(8,128)(2,1)}, f32[128,512]{1,0:T(8,128)}) custom-call(bf16[128,512]{1,0:T(8,128)(2,1)} %tok_ref.1, s32[8,128]{1,0:T(8,128)} %bitcast.1, s32[128,8]{1,0:T(8,128)} %copy.8.ids_ref, f32[128,8]{1,0:T(8,128)} %copy.9.route_ref, bf16[2,192,4096]{2,1,0:T(8,128)(2,1)} %gate_hbm.1, bf16[2,192,4096]{2,1,0:T(8,128)(2,1)} %up_hbm.1, ...), custom_call_target="tpu_custom_call" | custom-call | tf_op jit(solution)/shard_map/moe_layer/pallas_call | solution.py:656
  185.1 1.6 copy.12
  186.6 1.7 copy.13

commit v2 on v1

v2 whole, which is shorter than its diff:
```python
import functools

import jax
import jax.numpy as jnp
from jax import lax
from jax.experimental import pallas as pl
from jax.experimental.pallas import tpu as pltpu
from jax.sharding import PartitionSpec as P

MESH = pl.DeviceIdType.MESH
CAP = 20
HEAD = 16
REST = CAP - HEAD
BF = jnp.bfloat16
F32 = jnp.float32
COEF = (6.5788915972740805, -12.960054087409885, 11.90224462767755, -5.297839452865238)
ROUND = 12582912.0


def soft_level(values):
    whole = (values + ROUND) - ROUND
    rest = values - whole
    square = rest * rest
    poly = COEF[-1]
    for coef in COEF[-2::-1]:
        poly = poly * square + coef
    return whole + (rest * square) * poly


def dot_nt(a, b):
    return lax.dot_general(a, b, (((1,), (1,)), ((), ())), preferred_element_type=F32)


def dot_nn(a, b):
    return lax.dot_general(a, b, (((1,), (0,)), ((), ())), preferred_element_type=F32)


def iota(shape, axis):
    return lax.broadcasted_iota(jnp.int32, shape, axis)


def layer_kernel(
    groups,
    ring,
    tok_ref,
    ids_t_ref,
    route_ref,
    gate_hbm,
    up_hbm,
    down_hbm,
    quant_ref,
    float_ref,
    tok,
    send_head,
    send_rest,
    rows,
    rest_in,
    weight,
    weight_q,
    down,
    down_q,
    rows_q,
    acc_float,
    acc_quant,
    hid_float,
    hid_quant,
    hid_level,
    peak_own,
    peak_in,
    smooth,
    inv_smooth,
    row_peak,
    row_mul,
    row_div,
    level_div,
    col_mul,
    col_div,
    top_send,
    top_in,
    mix_head,
    mix_rest,
    outf_head,
    outf_rest,
    outq_head,
    outq_rest,
    rest_acc,
    backf_head,
    backf_rest,
    backq_head,
    backq_rest,
    part,
    part_in,
    load_sem,
    swap_send,
    swap_recv,
    a2a_send,
    a2a_recv,
    small_send,
    small_recv,
    ring_send,
    ring_recv,
    ex_send,
    ex_recv,
):
    me = lax.axis_index("dp")
    seat = lax.axis_index("expert")
    x = seat // 2
    core = seat % 2
    width = tok_ref.shape[1]
    wide = 2 * width
    quarter = wide // 4
    hid = gate_hbm.shape[1]
    hid2 = 2 * hid
    count = groups * CAP
    half = count // 2
    n_head = groups * HEAD
    gh = groups // 2
    half_head = gh * HEAD
    piece_rows = half // 2
    top = ids_t_ref.shape[0]
    toks = tok_ref.shape[0]
    lanes = min(512, wide)
    block = 128 if count % 128 == 0 else count
    n_block = count // block
    hidden_all = ring * hid2

    partner = (me, x * 2 + 1 - core)

    def along(k):
        return (me, lax.rem(x + k, ring) * 2 + core)

    def peer(k):
        return (lax.rem(me + k, groups), seat)

    loads = []
    for s in range(ring):
        for g, src in enumerate((gate_hbm, up_hbm)):
            loads.append(
                pltpu.make_async_copy(
                    src.at[core, :, pl.ds(s * wide, wide)],
                    weight.at[s, pl.ds(pl.multiple_of(g * hid2 + core * hid, 8), hid), :],
                    load_sem.at[2 * s + g],
                )
            )
    loads.append(
        pltpu.make_async_copy(
            down_hbm.at[core],
            down.at[:, pl.ds(pl.multiple_of(core * width, 128), width)],
            load_sem.at[2 * ring],
        )
    )
    loads[-1].start()
    for copy in loads[:-1]:
        copy.start()

    barrier = pltpu.get_barrier_semaphore()
    pl.semaphore_signal(barrier, inc=1, device_id=partner, device_id_type=MESH)
    for k in range(1, ring):
        pl.semaphore_signal(barrier, inc=1, device_id=along(k), device_id_type=MESH)

    def greet(k, carry):
        pl.semaphore_signal(barrier, inc=1, device_id=peer(k), device_id_type=MESH)
        return carry

    lax.fori_loop(1, groups, greet, 0)

    before = (iota((toks, toks), 0) < iota((toks, toks), 1)).astype(BF)
    row_id = iota((n_head, toks), 0)
    hit = jnp.zeros((n_head, toks), F32)
    wanted = (row_id // HEAD) * 2 + core
    share = jnp.zeros((n_head, toks), F32)
    ratio = route_ref[...]
    ratio = ratio / jnp.sum(ratio, axis=0, keepdims=True)
    for k in range(top):
        same = ids_t_ref[k : k + 1, :] == wanted
        hit = hit + same.astype(F32)
        share = share + jnp.where(same, ratio[k : k + 1, :], 0.0)
    slot = dot_nn(hit.astype(BF), before)
    pick_head = jnp.where(slot == (row_id % HEAD).astype(F32), hit, 0.0).astype(BF)
    pick_rest = jnp.where(slot == (HEAD + row_id % REST).astype(F32), hit, 0.0)
    part_id = (row_id // REST) % 4
    hit_group = jnp.zeros((groups, toks), F32)
    wanted = iota((groups, toks), 0) * 2 + core
    for k in range(top):
        hit_group = hit_group + (ids_t_ref[k : k + 1, :] == wanted).astype(F32)
    slot_group = dot_nn(hit_group.astype(BF), before)
    pick_all = jnp.concatenate(
        [jnp.where(slot_group == float(n), hit_group, 0.0).astype(BF) for n in range(CAP)], axis=0
    )
    tiles = wide // 128
    eighth = quarter // 2
    middle = wide // 2

    pl.semaphore_wait(barrier, 1 + (ring - 1) + (groups - 1))

    own_cols = pl.ds(pl.multiple_of(core * width, 128), width)
    tok_copy = pltpu.make_async_remote_copy(
        src_ref=tok_ref,
        dst_ref=tok.at[:, own_cols],
        send_sem=swap_send.at[0],
        recv_sem=swap_recv.at[0],
        device_id=partner,
        device_id_type=MESH,
    )
    tok_copy.start()
    tok[:, own_cols] = tok_ref[...]
    swaps = [
        pltpu.make_async_remote_copy(
            src_ref=down_hbm.at[1 - core],
            dst_ref=down.at[:, own_cols],
            send_sem=swap_send.at[1],
            recv_sem=swap_recv.at[1],
            device_id=partner,
            device_id_type=MESH,
        )
    ]
    for s in range(ring):
        for g, src in enumerate((gate_hbm, up_hbm)):
            swaps.append(
                pltpu.make_async_remote_copy(
                    src_ref=src.at[1 - core, :, pl.ds(s * wide, wide)],
                    dst_ref=weight.at[s, pl.ds(pl.multiple_of(g * hid2 + core * hid, 8), hid), :],
                    send_sem=swap_send.at[2 + 2 * s + g],
                    recv_sem=swap_recv.at[2 + 2 * s + g],
                    device_id=partner,
                    device_id_type=MESH,
                )
            )
    tok_copy.wait()
    for copy in swaps:
        copy.start()

    every = jnp.abs(dot_nn(pick_all, tok[...]))
    highest = every[0:groups]
    for n in range(1, CAP):
        highest = jnp.maximum(highest, every[n * groups : (n + 1) * groups])
    for n in range(tiles):
        top_send[pl.ds(n, groups, stride=tiles), :] = highest[:, n * 128 : (n + 1) * 128]

    def top_at(g):
        return pl.ds(pl.multiple_of(g * tiles, tiles), tiles)

    def send_top(k, carry):
        pltpu.make_async_remote_copy(
            src_ref=top_send.at[top_at(lax.rem(me + k, groups)), :],
            dst_ref=top_in.at[top_at(me), :],
            send_sem=a2a_send.at[4, 0],
            recv_sem=a2a_recv.at[4, 0],
            device_id=peer(k),
            device_id_type=MESH,
        ).start()
        return carry

    lax.fori_loop(1, groups, send_top, 0)
    top_in[top_at(me), :] = top_send[top_at(me), :]

    send_head[...] = dot_nn(pick_head, tok[...]).astype(BF)
    chosen = jnp.zeros((n_head, quarter), F32)
    for q in range(4):
        pair = jnp.concatenate(
            (
                tok[:, q * eighth : (q + 1) * eighth],
                tok[:, middle + q * eighth : middle + (q + 1) * eighth],
            ),
            axis=1,
        )
        chosen = chosen + dot_nn(jnp.where(part_id == q, pick_rest, 0.0).astype(BF), pair)
    send_rest[...] = chosen.astype(BF)

    def at_group(g):
        return pl.ds(pl.multiple_of(g * HEAD, HEAD), HEAD)

    def split_group(g):
        return pl.ds(pl.multiple_of((g % 2) * half_head + (g // 2) * HEAD, HEAD), HEAD)

    def landing_group(g):
        return pl.ds(pl.multiple_of((g % 2) * half + (g // 2) * HEAD, HEAD), HEAD)

    def remote(number, index, src, dst, k):
        return pltpu.make_async_remote_copy(
            src_ref=src,
            dst_ref=dst,
            send_sem=a2a_send.at[number, index],
            recv_sem=a2a_recv.at[number, index],
            device_id=peer(k),
            device_id_type=MESH,
        )

    total = pl.ds(0, (groups - 1) * HEAD)

    slab = rows.at[x]

    sent = []
    for side in range(2):
        cols = slice(side * middle, (side + 1) * middle)
        thin = slice(side * eighth, (side + 1) * eighth)
        number = 3 * side

        def dispatch(k, carry):
            to = at_group(lax.rem(me + k, groups))
            remote(number, 0, send_head.at[to, cols], slab.at[landing_group(me), cols], k).start()
            remote(number, 1, send_rest.at[to, thin], rest_in.at[at_group(me), thin], k).start()
            return carry

        lax.fori_loop(1, groups, dispatch, 0)
        sent.append(
            (
                remote(number, 0, send_head.at[total, cols], slab.at[total, cols], 1),
                remote(number, 1, send_rest.at[total, thin], rest_in.at[total, thin], 1),
            )
        )
    slab[landing_group(me), :] = send_head[at_group(me), :]
    rest_in[at_group(me), :] = send_rest[at_group(me), :]

    def send_back(number, part_of, src_head, src_rest, dst_head, dst_rest):
        def begin(i, carry):
            to = 2 * lax.rem(me // 2 + i, gh) + part_of

            @pl.when(to != me)
            def _():
                at = split_group(to)
                k = to - me + groups
                remote(number, 0, src_head.at[at, :], dst_head.at[at_group(me), :], k).start()
                remote(number, 1, src_rest.at[at, :], dst_rest.at[at_group(me), :], k).start()

            return carry

        lax.fori_loop(1, gh + 1, begin, 0)

        @pl.when(me % 2 == part_of)
        def _():
            dst_head[at_group(me), :] = src_head[split_group(me), :]
            dst_rest[at_group(me), :] = src_rest[split_group(me), :]

    def back(number, src_head, src_rest, dst_head, dst_rest):
        return (
            remote(number, 0, src_head.at[total, :], dst_head.at[total, :], 1),
            remote(number, 1, src_rest.at[total, :], dst_rest.at[total, :], 1),
        )

    for which, ref in (
        ((row_id % HEAD).astype(F32), mix_head),
        ((HEAD + row_id % REST).astype(F32), mix_rest),
    ):
        value = jnp.where(slot == which, share, 0.0).T
        high = value.astype(BF)
        ref[0:toks, :] = high
        ref[toks:, :] = (value - high.astype(F32)).astype(BF)

    loads[-1].wait()
    swaps[0].wait()
    for n in range(wide // lanes):
        cols = slice(n * lanes, (n + 1) * lanes)

        def down_peak(i, best):
            at = pl.ds(pl.multiple_of(i * 16, 16), 16)
            return jnp.maximum(best, jnp.abs(down[at, cols].astype(F32)))

        best = lax.fori_loop(0, hidden_all // 16, down_peak, jnp.zeros((16, lanes), F32))
        peak = jnp.max(best, axis=0, keepdims=True) + 1e-06
        col_mul[:, cols] = jnp.broadcast_to(7.0 / peak, (8, lanes))
        col_div[:, cols] = jnp.broadcast_to(peak / 7.0, (8, lanes))

        def down_level(i, carry):
            at = pl.ds(pl.multiple_of(i * 16, 16), 16)
            value = down[at, cols].astype(F32)
            mul = jnp.concatenate((col_mul[:, cols], col_mul[:, cols]), axis=0)
            down_q[at, cols] = soft_level(value * mul).astype(BF)
            return carry

        lax.fori_loop(0, hidden_all // 16, down_level, 0)

    for s in range(ring):
        loads[2 * s].wait()
        loads[2 * s + 1].wait()
        swaps[1 + 2 * s].wait()
        swaps[2 + 2 * s].wait()
        for n in range(wide // lanes):
            cols = slice(n * lanes, (n + 1) * lanes)

            def weight_top(i, best):
                at = pl.ds(pl.multiple_of(i * 16, 16), 16)
                return jnp.maximum(best, jnp.abs(weight[s, at, cols].astype(F32)))

            best = lax.fori_loop(0, 2 * hid2 // 16, weight_top, jnp.zeros((16, lanes), F32))
            peak_own[s, :, cols] = jnp.broadcast_to(jnp.max(best, axis=0, keepdims=True), (8, lanes))

    def small(number, k, src, dst):
        return pltpu.make_async_remote_copy(
            src_ref=src,
            dst_ref=dst,
            send_sem=small_send.at[number, k - 1],
            recv_sem=small_recv.at[number, k - 1],
            device_id=along(k),
            device_id_type=MESH,
        )

    peak_copies = [
        small(0, k, peak_own.at[lax.rem(x + k, ring)], peak_in.at[k - 1]) for k in range(1, ring)
    ]
    for copy in peak_copies:
        copy.start()
    for copy in peak_copies:
        copy.wait()
    weight_peak = peak_own[x]
    for k in range(1, ring):
        weight_peak = jnp.maximum(weight_peak, peak_in[k - 1])

    def ring_copy(number, ref, h, way, step, mag, to):
        if way == 0:
            owner = lax.rem(x - mag + ring, ring)
            part_of = step % 2
        else:
            owner = lax.rem(x + mag, ring)
            part_of = 1 - step % 2
        at = pl.ds(h * half + part_of * piece_rows, piece_rows)
        if ref is rows:
            piece = ref.at[owner, at, pl.ds((number // 3) * middle, middle)]
        else:
            piece = ref.at[owner, at, :]
        return pltpu.make_async_remote_copy(
            src_ref=piece,
            dst_ref=piece,
            send_sem=ring_send.at[number, h, way, step],
            recv_sem=ring_recv.at[number, h, way, step],
            device_id=along(to),
            device_id_type=MESH,
        )

    def hop(number, ref, h, way, step):
        return ring_copy(number, ref, h, way, step, step // 2, 1 if way == 0 else ring - 1)

    def landed(number, ref, h, way, step):
        return ring_copy(number, ref, h, way, step, 1 + step // 2, 1)

    def launch(number, ref, h, steps):
        for step in steps:
            for way in range(2):
                hop(number, ref, h, way, step).start()

    def await_step(number, ref, h, step):
        for way in range(2):
            landed(number, ref, h, way, step).wait_recv()

    def relay(number, ref, h):
        for way in range(2):
            landed(number, ref, h, way, 0).wait_recv()
            hop(number, ref, h, way, 2).start()

    def drain(number, ref):
        for h in range(2):
            for step in range(3):
                for way in range(2):
                    hop(number, ref, h, way, step).wait_send()

    pltpu.make_async_remote_copy(
        src_ref=top_send.at[pl.ds(0, (groups - 1) * tiles), :],
        dst_ref=top_in.at[pl.ds(0, (groups - 1) * tiles), :],
        send_sem=a2a_send.at[4, 0],
        recv_sem=a2a_recv.at[4, 0],
        device_id=peer(1),
        device_id_type=MESH,
    ).wait()
    act_peak = top_in[0:tiles, :]
    for g in range(1, groups):
        act_peak = jnp.maximum(act_peak, top_in[g * tiles : (g + 1) * tiles, :])
    act_peak = jnp.maximum(act_peak, 1.0)
    for n in range(tiles):
        cols = slice(n * 128, (n + 1) * 128)
        smooth[x, :, cols] = jnp.sqrt(act_peak[n : n + 1, :] / (weight_peak[:, cols] + 1e-06))
    smooth_copies = [small(1, k, smooth.at[x], smooth.at[x]) for k in range(1, ring)]
    for copy in smooth_copies:
        copy.start()
    for copy in smooth_copies:
        copy.wait()
    for s in range(ring):
        inv_smooth[s, :, :] = 1.0 / smooth[s]

    spread = iota((gh * REST, n_head), 1)
    home = iota((gh * REST, n_head), 0)

    def arrive(side):
        for copy in sent[side]:
            copy.wait_send()
            copy.wait_recv()
        for h in range(2):
            same_row = (spread // HEAD == 2 * (home // REST) + h) & (spread % REST == home % REST)
            for q in range(4):
                order = (same_row & ((spread // REST) % 4 == q)).astype(F32).astype(BF)
                slab[
                    h * half + half_head : (h + 1) * half,
                    side * middle + q * eighth : side * middle + (q + 1) * eighth,
                ] = dot_nn(order, rest_in[:, side * eighth : (side + 1) * eighth]).astype(BF)

    arrive(0)
    launch(0, rows, 0, (0, 1))

    def weight_level(i, carry):
        at = pl.ds(pl.multiple_of(i * 16, 16), 16)
        best = jnp.zeros((16, lanes), F32)
        for s in range(ring):
            for n in range(wide // lanes):
                cols = slice(n * lanes, (n + 1) * lanes)
                best = jnp.maximum(best, jnp.abs(weight[s, at, cols].astype(F32) * smooth[s, 0:1, cols]))
        peak = jnp.max(best, axis=1, keepdims=True) + 1e-06
        mul = 7.0 / peak
        div = peak / 7.0
        for s in range(ring):
            for n in range(wide // lanes):
                cols = slice(n * lanes, (n + 1) * lanes)
                value = weight[s, at, cols].astype(F32) * smooth[s, 0:1, cols]
                weight_q[s, at, cols] = (div * soft_level(value * mul)).astype(BF)
        return carry

    n_strip = 2 * hid2 // 16
    lax.fori_loop(0, n_strip // 2, weight_level, 0)
    relay(0, rows, 0)
    launch(0, rows, 1, (0,))
    lax.fori_loop(n_strip // 2, n_strip, weight_level, 0)

    arrive(1)
    eye = iota((block, block), 0) == iota((block, block), 1)
    top_rows = []
    for b in range(n_block):
        best = jnp.zeros((block, 128), F32)
        for n in range(tiles):
            cols = slice(n * 128, (n + 1) * 128)
            value = rows[x, b * block : (b + 1) * block, cols].astype(F32) * inv_smooth[x, 0:1, cols]
            best = jnp.maximum(best, jnp.abs(value))
        tall = jnp.max(best, axis=1, keepdims=True)
        top_rows.append(jnp.sum(jnp.where(eye, tall, 0.0), axis=0, keepdims=True))
    row_peak[x] = jnp.zeros((8, block), F32)
    for b in range(n_block):
        row_peak[x, b : b + 1, :] = top_rows[b]
    peak_rows = [small(2, k, row_peak.at[x], row_peak.at[x]) for k in range(1, ring)]
    for copy in peak_rows:
        copy.start()
    launch(3, rows, 0, (0, 1))

    strip = 16 if half % 16 == 0 else half

    def use_float(owner, h, first):
        at = pl.ds(h * half, half)
        product = dot_nt(rows[owner, at, :], weight[owner])
        acc_float[at, :] = product if first else acc_float[at, :] + product

    def use_quant(owner, h, first):
        at = pl.ds(h * half, half)

        def row_level(i, carry):
            here = pl.ds(h * half + i * strip, strip)
            out = pl.ds(i * strip, strip)
            mul = row_mul[here, 0:1]
            div = row_div[here, 0:1]
            for n in range(wide // lanes):
                cols = slice(n * lanes, (n + 1) * lanes)
                value = rows[owner, here, cols].astype(F32) * inv_smooth[owner, 0:1, cols]
                rows_q[out, cols] = (div * soft_level(value * mul)).astype(BF)
            return carry

        lax.fori_loop(0, half // strip, row_level, 0)
        product = dot_nt(rows_q[...], weight_q[owner])
        acc_quant[at, :] = product if first else acc_quant[at, :] + product

    def use_others(h):
        def one(i, carry):
            @pl.when(i == 0)
            def _():
                await_step(0, rows, h, 1)
                await_step(3, rows, h, 1)

            @pl.when(i == 2)
            def _():
                await_step(0, rows, h, 2)
                await_step(3, rows, h, 2)

            owner = lax.rem(x + ring - 1 + 2 * (i % 2) + 3 * (i // 2), ring)
            use_float(owner, h, False)
            use_quant(owner, h, False)
            return carry

        lax.fori_loop(0, ring - 1, one, 0)

    def activate(acc, out, h):
        def piece(i, carry):
            at = pl.ds(pl.multiple_of(h * half + i * strip, strip), strip)
            gate = acc[at, 0:hid2]
            up = acc[at, hid2:]
            out[x, at, :] = (gate / (1.0 + jnp.exp(-gate)) * up).astype(BF)
            return carry

        lax.fori_loop(0, half // strip, piece, 0)

    turn = iota((half_head, gh * REST), 0)
    base = iota((half_head, gh * REST), 1)
    back_row = (turn // HEAD == base // REST) & (turn % REST == base % REST)
    turn_part = (turn // REST) % 4

    def project(hidden, matrix, head, rest, h, scaled):
        rest_acc[...] = jnp.zeros_like(rest_acc)
        at = pl.ds(h * half, half)

        def piece(q, carry):
            cols = pl.ds(pl.multiple_of(q * quarter, quarter), quarter)
            total = dot_nn(hidden[0, at, :], matrix[0:hid2, cols])
            for s in range(1, ring):
                total = total + dot_nn(hidden[s, at, :], matrix[s * hid2 : (s + 1) * hid2, cols])
            if scaled:
                total = total * level_div[at, 0:1] * col_div[0:1, cols]
            total = total.astype(BF)
            head[h * half_head : (h + 1) * half_head, cols] = total[:half_head]
            order = (back_row & (turn_part == q)).astype(F32).astype(BF)
            rest_acc[...] += dot_nn(order, total[half_head:])
            return carry

        lax.fori_loop(0, 4, piece, 0)
        rest[h * half_head : (h + 1) * half_head, :] = rest_acc[...].astype(BF)

    def levels(h):
        def piece(i, carry):
            at = pl.ds(pl.multiple_of(h * half + i * strip, strip), strip)
            best = jnp.zeros((strip, hid2), F32)
            for s in range(ring):
                best = jnp.maximum(best, jnp.abs(hid_quant[s, at, :].astype(F32)))
            peak = jnp.max(best, axis=1, keepdims=True) + 1e-06
            mul = 7.0 / peak
            level_div[at, :] = jnp.broadcast_to(peak / 7.0, (strip, 128))
            for s in range(ring):
                hid_level[s, at, :] = soft_level(hid_quant[s, at, :].astype(F32) * mul).astype(BF)
            return carry

        lax.fori_loop(0, half // strip, piece, 0)

    use_float(x, 0, True)
    for copy in peak_rows:
        copy.wait()
    best_row = row_peak[0]
    for s in range(1, ring):
        best_row = jnp.maximum(best_row, row_peak[s])
    for b in range(n_block):
        flat = jnp.broadcast_to(best_row[b : b + 1, :], (block, block))
        tall = jnp.sum(jnp.where(eye, flat, 0.0), axis=1, keepdims=True) + 1e-06
        row_mul[b * block : (b + 1) * block, :] = jnp.broadcast_to(7.0 / tall, (block, 128))
        row_div[b * block : (b + 1) * block, :] = jnp.broadcast_to(tall / 7.0, (block, 128))
    use_quant(x, 0, True)
    relay(3, rows, 0)
    launch(0, rows, 1, (1,))
    relay(0, rows, 1)
    use_float(x, 1, True)
    launch(3, rows, 1, (0,))
    use_others(0)
    activate(acc_float, hid_float, 0)
    launch(1, hid_float, 0, (0, 1))
    activate(acc_quant, hid_quant, 0)
    launch(2, hid_quant, 0, (0, 1))
    use_quant(x, 1, True)
    relay(1, hid_float, 0)
    relay(2, hid_quant, 0)
    launch(3, rows, 1, (1,))
    relay(3, rows, 1)
    await_step(1, hid_float, 0, 1)
    await_step(1, hid_float, 0, 2)
    project(hid_float, down, outf_head, outf_rest, 0, False)
    send_back(1, 0, outf_head, outf_rest, backf_head, backf_rest)
    await_step(2, hid_quant, 0, 1)
    await_step(2, hid_quant, 0, 2)
    levels(0)
    project(hid_level, down_q, outq_head, outq_rest, 0, True)
    send_back(2, 0, outq_head, outq_rest, backq_head, backq_rest)
    use_others(1)
    activate(acc_float, hid_float, 1)
    launch(1, hid_float, 1, (0, 1))
    activate(acc_quant, hid_quant, 1)
    relay(1, hid_float, 1)
    launch(2, hid_quant, 1, (0, 1))
    await_step(1, hid_float, 1, 1)
    await_step(1, hid_float, 1, 2)
    project(hid_float, down, outf_head, outf_rest, 1, False)
    send_back(1, 1, outf_head, outf_rest, backf_head, backf_rest)
    relay(2, hid_quant, 1)
    await_step(2, hid_quant, 1, 1)
    await_step(2, hid_quant, 1, 2)
    levels(1)
    project(hid_level, down_q, outq_head, outq_rest, 1, True)
    send_back(2, 1, outq_head, outq_rest, backq_head, backq_rest)
    sent_float = back(1, outf_head, outf_rest, backf_head, backf_rest)
    sent_quant = back(2, outq_head, outq_rest, backq_head, backq_rest)

    def combine(number, head, rest):
        mixed = dot_nn(mix_head[...], head[...])
        mixed = mixed[:toks] + mixed[toks:]
        quarter_of = (iota((2 * toks, n_head), 1) // REST) % 4
        for q in range(4):
            weights = jnp.where(quarter_of == q, mix_rest[...].astype(F32), 0.0).astype(BF)
            extra = dot_nn(weights, rest[...])
            cols = slice(q * quarter, (q + 1) * quarter)
            first = (q * quarter) // width
            inner = q * quarter - first * width
            part[number, first, :, inner : inner + quarter] = mixed[:, cols] + extra[:toks] + extra[toks:]
        copy = pltpu.make_async_remote_copy(
            src_ref=part.at[number, 1 - core],
            dst_ref=part_in.at[number],
            send_sem=ex_send.at[number],
            recv_sem=ex_recv.at[number],
            device_id=partner,
            device_id_type=MESH,
        )
        copy.start()
        return copy

    for copy in sent_float:
        copy.wait_recv()
    half_float = combine(0, backf_head, backf_rest)
    half_float.wait()
    float_ref[...] = part[0, core] + part_in[0]
    for copy in sent_quant:
        copy.wait_recv()
    half_quant = combine(1, backq_head, backq_rest)

    for copy in sent_float:
        copy.wait_send()
    for copy in sent_quant:
        copy.wait_send()
    for number, ref in enumerate((rows, hid_float, hid_quant, rows)):
        drain(number, ref)
    half_quant.wait()
    quant_ref[...] = (part[1, core] + part_in[1]).astype(BF)


def solution(mesh):
    groups = mesh.shape["dp"]
    ring = mesh.shape["expert"] // 2

    def on_device(tokens, expert_ids, route_weights, gate_weight, up_weight, down_weight):
        toks, width = tokens.shape
        wide = 2 * width
        quarter = wide // 4
        hid = gate_weight.shape[1]
        hid2 = 2 * hid
        count = groups * CAP
        half = count // 2
        n_head = groups * HEAD
        hidden_all = ring * hid2
        block = 128 if count % 128 == 0 else count
        vmem = pltpu.VMEM
        dma = pltpu.SemaphoreType.DMA
        here = pl.BlockSpec(memory_space=pltpu.VMEM)
        away = pl.BlockSpec(memory_space=pl.ANY)
        return pl.pallas_call(
            functools.partial(layer_kernel, groups, ring),
            name="moe_layer",
            out_shape=(
                jax.ShapeDtypeStruct((toks, width), BF),
                jax.ShapeDtypeStruct((toks, width), F32),
            ),
            in_specs=[here, here, here, away, away, away],
            out_specs=(here, here),
            scratch_shapes=[
                vmem((toks, wide), BF),
                vmem((n_head, wide), BF),
                vmem((n_head, quarter), BF),
                vmem((ring, count, wide), BF),
                vmem((n_head, quarter), BF),
                vmem((ring, 2 * hid2, wide), BF),
                vmem((ring, 2 * hid2, wide), BF),
                vmem((hidden_all, wide), BF),
                vmem((hidden_all, wide), BF),
                vmem((half, wide), BF),
                vmem((count, 2 * hid2), F32),
                vmem((count, 2 * hid2), F32),
                vmem((ring, count, hid2), BF),
                vmem((ring, count, hid2), BF),
                vmem((ring, count, hid2), BF),
                vmem((ring, 8, wide), F32),
                vmem((ring - 1, 8, wide), F32),
                vmem((ring, 8, wide), F32),
                vmem((ring, 8, wide), F32),
                vmem((ring, 8, block), F32),
                vmem((count, 128), F32),
                vmem((count, 128), F32),
                vmem((count, 128), F32),
                vmem((8, wide), F32),
                vmem((8, wide), F32),
                vmem((groups * (wide // 128), 128), F32),
                vmem((groups * (wide // 128), 128), F32),
                vmem((2 * toks, n_head), BF),
                vmem((2 * toks, n_head), BF),
                vmem((n_head, wide), BF),
                vmem((n_head, quarter), BF),
                vmem((n_head, wide), BF),
                vmem((n_head, quarter), BF),
                vmem((n_head // 2, quarter), F32),
                vmem((n_head, wide), BF),
                vmem((n_head, quarter), BF),
                vmem((n_head, wide), BF),
                vmem((n_head, quarter), BF),
                vmem((2, 2, toks, width), F32),
                vmem((2, toks, width), F32),
                dma((2 * ring + 1,)),
                dma((2 + 2 * ring,)),
                dma((2 + 2 * ring,)),
                dma((5, 2)),
                dma((5, 2)),
                dma((3, ring - 1)),
                dma((3, ring - 1)),
                dma((4, 2, 2, 3)),
                dma((4, 2, 2, 3)),
                dma((2,)),
                dma((2,)),
            ],
            compiler_params=pltpu.CompilerParams(
                collective_id=0, has_side_effects=True, vmem_limit_bytes=64 * 1024 * 1024 - 128 * 1024
            ),
        )(
            tokens,
            expert_ids.T,
            route_weights.T,
            gate_weight,
            up_weight,
            down_weight,
        )

    in_specs = (
        P("dp", "expert"),
        P("dp", None),
        P("dp", None),
        P("dp", "expert", None),
        P("dp", "expert", None),
        P("dp", None, "expert"),
    )
    out_specs = (P("dp", "expert"), P("dp", "expert"))
    return jax.shard_map(
        on_device, mesh=mesh, in_specs=in_specs, out_specs=out_specs, check_vma=False
    )
```

time: 192 us -> 166 us (0.86); the launches traced: 188 us -> 166 us
  Pallas kernels: 182 us -> 162 us
  local copies, waits for them, and re-layouts: 6.07 us -> 3.24 us
    pallas_call x1, Pallas kernels: 182 us -> 162 us  [on_device(): pl.pallas_call(functools.partial(layer_kernel, groups, ring), name='moe_l...]
    unnamed x4 -> x2, local copies, waits for them, and re-layouts: 6.07 us -> 3.24 us
where the time goes in v2:
time: 166 us
  Pallas kernels  162 us (98%)
  local copies, waits for them, and re-layouts  3.24 us (2%)
    pallas_call x1, Pallas kernels, on_device(): pl.pallas_call(functools.partial(layer_kernel, groups, ring), name='moe_l...  162 us

profile of v2, /device:TPU:33, one launch (start us, length us, event | category | flops | bytes accessed | tf_op | source)
XLA Modules:
  0.0 166.3 jit_solution(7890930929995023887)
XLA Ops:
  0.6 162.4 %moe_layer.1 = (bf16[128,512]{1,0:T(8,128)(2,1)}, f32[128,512]{1,0:T(8,128)}) custom-call(bf16[128,512]{1,0:T(8,128)(2,1)} %tok_ref.1, s32[8,128]{1,0:T(8,128)} %bitcast.2, f32[8,128]{1,0:T(8,128)} %bitcast.3, bf16[2,192,4096]{2,1,0:T(8,128)(2,1)} %gate_hbm.1, bf16[2,192,4096]{2,1,0:T(8,128)(2,1)} %up_hbm.1, bf16[2,1536,512]{2,1,0:T(8,128)(2,1)} %down_hbm.1), custom_call_target="tpu_custom_call" | custom-call | tf_op jit(solution)/shard_map/moe_layer/pallas_call | solution.py:749
  163.0 1.6 copy.10
  164.6 1.7 %copy.11 = f32[128,512]{1,0:T(8,128)} copy(f32[128,512]{1,0:T(8,128)} %get-tuple-element.5) | data formatting | bytes 524288

commit v3 on v2

--- a/solution.py
+++ b/solution.py
@@ -48,8 +48,7 @@
     gate_hbm,
     up_hbm,
     down_hbm,
-    quant_ref,
-    float_ref,
+    both_ref,
     tok,
     send_head,
     send_rest,
@@ -60,6 +59,7 @@
     down,
     down_q,
     rows_q,
+    rows_q2,
     acc_float,
     acc_quant,
     hid_float,
@@ -90,6 +90,14 @@
     backq_rest,
     part,
     part_in,
+    tok_far,
+    far_head,
+    far_rest,
+    far_in,
+    tok_send,
+    tok_recv,
+    far_send,
+    far_recv,
     load_sem,
     swap_send,
     swap_recv,
@@ -227,6 +235,23 @@
                 )
             )
     tok_copy.wait()
+    odd = (me + me // 8) % 2 == 1
+
+    def far_tokens(k):
+        return pltpu.make_async_remote_copy(
+            src_ref=tok.at[:, pl.ds(wide // 2, wide // 2)],
+            dst_ref=tok_far.at[k - 1],
+            send_sem=tok_send.at[k - 1],
+            recv_sem=tok_recv.at[k - 1],
+            device_id=along(k),
+            device_id_type=MESH,
+        )
+
+    @pl.when(odd)
+    def _():
+        for k in range(1, ring):
+            far_tokens(k).start()
+
     for copy in swaps:
         copy.start()
 
@@ -267,14 +292,17 @@
         chosen = chosen + dot_nn(jnp.where(part_id == q, pick_rest, 0.0).astype(BF), pair)
     send_rest[...] = chosen.astype(BF)
 
+    def side_of(g):
+        return (g + g // 8) % 2
+
     def at_group(g):
         return pl.ds(pl.multiple_of(g * HEAD, HEAD), HEAD)
 
     def split_group(g):
-        return pl.ds(pl.multiple_of((g % 2) * half_head + (g // 2) * HEAD, HEAD), HEAD)
+        return pl.ds(pl.multiple_of(side_of(g) * half_head + (g // 2) * HEAD, HEAD), HEAD)
 
     def landing_group(g):
-        return pl.ds(pl.multiple_of((g % 2) * half + (g // 2) * HEAD, HEAD), HEAD)
+        return pl.ds(pl.multiple_of(side_of(g) * half + (g // 2) * HEAD, HEAD), HEAD)
 
     def remote(number, index, src, dst, k):
         return pltpu.make_async_remote_copy(
@@ -314,7 +342,8 @@
 
     def send_back(number, part_of, src_head, src_rest, dst_head, dst_rest):
         def begin(i, carry):
-            to = 2 * lax.rem(me // 2 + i, gh) + part_of
+            pair = lax.rem(me // 2 + i, gh)
+            to = 2 * pair + (part_of + pair // 4) % 2
 
             @pl.when(to != me)
             def _():
@@ -327,7 +356,7 @@
 
         lax.fori_loop(1, gh + 1, begin, 0)
 
-        @pl.when(me % 2 == part_of)
+        @pl.when(side_of(me) == part_of)
         def _():
             dst_head[at_group(me), :] = src_head[split_group(me), :]
             dst_rest[at_group(me), :] = src_rest[split_group(me), :]
@@ -400,6 +429,71 @@
     ]
     for copy in peak_copies:
         copy.start()
+
+    def far_copy(slot, src, dst, k):
+        return pltpu.make_async_remote_copy(
+            src_ref=src,
+            dst_ref=dst,
+            send_sem=far_send.at[slot],
+            recv_sem=far_recv.at[slot],
+            device_id=peer(k),
+            device_id_type=MESH,
+        )
+
+    right_cols = slice(middle, wide)
+    far_own = pl.ds(pl.multiple_of((me // 2) * HEAD, HEAD), HEAD)
+
+    def far_owner(slot):
+        return lax.rem(x + ring - 1 - slot, ring)
+
+    @pl.when(odd)
+    def _():
+        for slot in range(ring - 1):
+            far_tokens(slot + 1).wait()
+            far_head[slot] = dot_nn(pick_head, tok_far[slot]).astype(BF)
+            extra = jnp.zeros((n_head, eighth), F32)
+            for q in range(4):
+                extra = extra + dot_nn(
+                    jnp.where(part_id == q, pick_rest, 0.0).astype(BF),
+                    tok_far[slot, :, q * eighth : (q + 1) * eighth],
+                )
+            far_rest[:, slot * eighth : (slot + 1) * eighth] = extra.astype(BF)
+
+        def far_dispatch(k, carry):
+            to = at_group(lax.rem(me + k, groups))
+            for slot in range(ring - 1):
+                far_copy(
+                    slot, far_head.at[slot, to, :], rows.at[far_owner(slot), landing_group(me), right_cols], k
+                ).start()
+            far_copy(ring - 1, far_rest.at[to, :], far_in.at[far_own, :], k).start()
+            return carry
+
+        lax.fori_loop(1, groups, far_dispatch, 0)
+        for slot in range(ring - 1):
+            rows[far_owner(slot), landing_group(me), right_cols] = far_head[slot, at_group(me), :]
+        far_in[far_own, :] = far_rest[at_group(me), :]
+
+    def far_arrive():
+        for parity in range(min(2, gh)):
+
+            @pl.when(side_of(me) == parity)
+            def _():
+                some = pl.ds(0, (gh - parity) * HEAD)
+                for slot in range(ring - 1):
+                    far_copy(slot, far_head.at[slot, some, :], rows.at[0, some, right_cols], 1).wait_recv()
+                far_copy(ring - 1, far_rest.at[some, :], far_in.at[some, :], 1).wait_recv()
+
+        near = iota((gh * REST, half_head), 1)
+        base_row = iota((gh * REST, half_head), 0)
+        same_row = (near // HEAD == base_row // REST) & (near % REST == base_row % REST)
+        for q in range(4):
+            order = (same_row & ((near // REST) % 4 == q)).astype(F32).astype(BF)
+            moved = dot_nn(order, far_in[...]).astype(BF)
+            for slot in range(ring - 1):
+                rows[
+                    far_owner(slot), half + half_head : 2 * half, middle + q * eighth : middle + (q + 1) * eighth
+                ] = moved[:, slot * eighth : (slot + 1) * eighth]
+
     for copy in peak_copies:
         copy.wait()
     weight_peak = peak_own[x]
@@ -448,7 +542,7 @@
             hop(number, ref, h, way, 2).start()
 
     def drain(number, ref):
-        for h in range(2):
+        for h in range(1 if number == 3 else 2):
             for step in range(3):
                 for way in range(2):
                     hop(number, ref, h, way, step).wait_send()
@@ -484,7 +578,7 @@
             copy.wait_send()
             copy.wait_recv()
         for h in range(2):
-            same_row = (spread // HEAD == 2 * (home // REST) + h) & (spread % REST == home % REST)
+            same_row = (spread // HEAD == 2 * (home // REST) + (h + home // (4 * REST)) % 2) & (spread % REST == home % REST)
             for q in range(4):
                 order = (same_row & ((spread // REST) % 4 == q)).astype(F32).astype(BF)
                 slab[
@@ -544,42 +638,40 @@
         product = dot_nt(rows[owner, at, :], weight[owner])
         acc_float[at, :] = product if first else acc_float[at, :] + product
 
-    def use_quant(owner, h, first):
-        at = pl.ds(h * half, half)
-
-        def row_level(i, carry):
-            here = pl.ds(h * half + i * strip, strip)
-            out = pl.ds(i * strip, strip)
+    def level_rows(owner, h, out):
+        for i in range(half // strip):
+            here = slice(h * half + i * strip, h * half + (i + 1) * strip)
             mul = row_mul[here, 0:1]
             div = row_div[here, 0:1]
             for n in range(wide // lanes):
                 cols = slice(n * lanes, (n + 1) * lanes)
                 value = rows[owner, here, cols].astype(F32) * inv_smooth[owner, 0:1, cols]
-                rows_q[out, cols] = (div * soft_level(value * mul)).astype(BF)
-            return carry
-
-        lax.fori_loop(0, half // strip, row_level, 0)
-        product = dot_nt(rows_q[...], weight_q[owner])
+                out[i * strip : (i + 1) * strip, cols] = (div * soft_level(value * mul)).astype(BF)
+
+    def use_quant(owner, h, first, buf):
+        at = pl.ds(h * half, half)
+        product = dot_nt(buf[...], weight_q[owner])
         acc_quant[at, :] = product if first else acc_quant[at, :] + product
 
     def use_others(h):
-        def one(i, carry):
-            @pl.when(i == 0)
-            def _():
-                await_step(0, rows, h, 1)
-                await_step(3, rows, h, 1)
-
-            @pl.when(i == 2)
-            def _():
-                await_step(0, rows, h, 2)
-                await_step(3, rows, h, 2)
-
-            owner = lax.rem(x + ring - 1 + 2 * (i % 2) + 3 * (i // 2), ring)
-            use_float(owner, h, False)
-            use_quant(owner, h, False)
-            return carry
-
-        lax.fori_loop(0, ring - 1, one, 0)
+        left = lax.rem(x + ring - 1, ring)
+        right = lax.rem(x + 1, ring)
+        across = lax.rem(x + 2, ring)
+        await_step(0, rows, h, 1)
+        if h == 0:
+            await_step(3, rows, h, 1)
+        use_float(left, h, False)
+        level_rows(left, h, rows_q)
+        use_float(right, h, False)
+        level_rows(right, h, rows_q2)
+        use_quant(left, h, False, rows_q)
+        use_quant(right, h, False, rows_q2)
+        await_step(0, rows, h, 2)
+        if h == 0:
+            await_step(3, rows, h, 2)
+        use_float(across, h, False)
+        level_rows(across, h, rows_q)
+        use_quant(across, h, False, rows_q)
 
     def activate(acc, out, h):
         def piece(i, carry):
@@ -632,6 +724,7 @@
         lax.fori_loop(0, half // strip, piece, 0)
 
     use_float(x, 0, True)
+    use_float(x, 1, True)
     for copy in peak_rows:
         copy.wait()
     best_row = row_peak[0]
@@ -642,31 +735,30 @@
         tall = jnp.sum(jnp.where(eye, flat, 0.0), axis=1, keepdims=True) + 1e-06
         row_mul[b * block : (b + 1) * block, :] = jnp.broadcast_to(7.0 / tall, (block, 128))
         row_div[b * block : (b + 1) * block, :] = jnp.broadcast_to(tall / 7.0, (block, 128))
-    use_quant(x, 0, True)
+    level_rows(x, 0, rows_q)
+    use_quant(x, 0, True, rows_q)
     relay(3, rows, 0)
     launch(0, rows, 1, (1,))
-    relay(0, rows, 1)
-    use_float(x, 1, True)
-    launch(3, rows, 1, (0,))
     use_others(0)
     activate(acc_float, hid_float, 0)
     launch(1, hid_float, 0, (0, 1))
     activate(acc_quant, hid_quant, 0)
+    level_rows(x, 1, rows_q)
+    use_quant(x, 1, True, rows_q)
+    relay(1, hid_float, 0)
     launch(2, hid_quant, 0, (0, 1))
-    use_quant(x, 1, True)
-    relay(1, hid_float, 0)
-    relay(2, hid_quant, 0)
-    launch(3, rows, 1, (1,))
-    relay(3, rows, 1)
+    relay(0, rows, 1)
     await_step(1, hid_float, 0, 1)
     await_step(1, hid_float, 0, 2)
     project(hid_float, down, outf_head, outf_rest, 0, False)
     send_back(1, 0, outf_head, outf_rest, backf_head, backf_rest)
+    relay(2, hid_quant, 0)
     await_step(2, hid_quant, 0, 1)
     await_step(2, hid_quant, 0, 2)
     levels(0)
     project(hid_level, down_q, outq_head, outq_rest, 0, True)
     send_back(2, 0, outq_head, outq_rest, backq_head, backq_rest)
+    far_arrive()
     use_others(1)
     activate(acc_float, hid_float, 1)
     launch(1, hid_float, 1, (0, 1))
@@ -712,7 +804,7 @@
         copy.wait_recv()
     half_float = combine(0, backf_head, backf_rest)
     half_float.wait()
-    float_ref[...] = part[0, core] + part_in[0]
+    both_ref[0] = part[0, core] + part_in[0]
     for copy in sent_quant:
         copy.wait_recv()
     half_quant = combine(1, backq_head, backq_rest)
@@ -721,10 +813,17 @@
         copy.wait_send()
     for copy in sent_quant:
         copy.wait_send()
+
+    @pl.when(odd)
+    def _():
+        for slot in range(ring - 1):
+            far_copy(slot, far_head.at[slot, total, :], far_head.at[slot, total, :], 1).wait_send()
+        far_copy(ring - 1, far_rest.at[total, :], far_rest.at[total, :], 1).wait_send()
+
     for number, ref in enumerate((rows, hid_float, hid_quant, rows)):
         drain(number, ref)
     half_quant.wait()
-    quant_ref[...] = (part[1, core] + part_in[1]).astype(BF)
+    both_ref[1] = part[1, core] + part_in[1]
 
 
 def solution(mesh):
@@ -746,15 +845,12 @@
         dma = pltpu.SemaphoreType.DMA
         here = pl.BlockSpec(memory_space=pltpu.VMEM)
         away = pl.BlockSpec(memory_space=pl.ANY)
-        return pl.pallas_call(
+        both = pl.pallas_call(
             functools.partial(layer_kernel, groups, ring),
             name="moe_layer",
-            out_shape=(
-                jax.ShapeDtypeStruct((toks, width), BF),
-                jax.ShapeDtypeStruct((toks, width), F32),
-            ),
+            out_shape=jax.ShapeDtypeStruct((2, toks, width), F32),
             in_specs=[here, here, here, away, away, away],
-            out_specs=(here, here),
+            out_specs=here,
             scratch_shapes=[
                 vmem((toks, wide), BF),
                 vmem((n_head, wide), BF),
@@ -765,6 +861,7 @@
                 vmem((ring, 2 * hid2, wide), BF),
                 vmem((hidden_all, wide), BF),
                 vmem((hidden_all, wide), BF),
+                vmem((half, wide), BF),
                 vmem((half, wide), BF),
                 vmem((count, 2 * hid2), F32),
                 vmem((count, 2 * hid2), F32),
@@ -796,6 +893,14 @@
                 vmem((n_head, quarter), BF),
                 vmem((2, 2, toks, width), F32),
                 vmem((2, toks, width), F32),
+                vmem((ring - 1, toks, wide // 2), BF),
+                vmem((ring - 1, n_head, wide // 2), BF),
+                vmem((n_head, (ring - 1) * quarter // 2), BF),
+                vmem((n_head // 2, (ring - 1) * quarter // 2), BF),
+                dma((ring - 1,)),
+                dma((ring - 1,)),
+                dma((ring,)),
+                dma((ring,)),
                 dma((2 * ring + 1,)),
                 dma((2 + 2 * ring,)),
                 dma((2 + 2 * ring,)),
@@ -819,6 +924,7 @@
             up_weight,
             down_weight,
         )
+        return both[1].astype(BF), both[0]
 
     in_specs = (
         P("dp", "expert"),

time: 166 us -> 147 us (0.89)
  Pallas kernels: 162 us -> 142 us
    pallas_call x1, Pallas kernels: 162 us -> 142 us  [on_device(): pl.pallas_call(functools.partial(layer_kernel, groups, ring), name='moe_l...]
    unnamed x2 -> x0, local copies, waits for them, and re-layouts: 3.24 us -> none
    squeeze x0 -> x1, local copies, waits for them, and re-layouts: none -> 1.67 us  [on_device(): return (both[1].astype(BF), both[0])]
where the time goes in v3:
time: 147 us; the launch traced here: 146 us
  Pallas kernels  142 us (97%)
  local copies, waits for them, and re-layouts  3.29 us (2%)
    pallas_call x1, Pallas kernels, on_device(): pl.pallas_call(functools.partial(layer_kernel, groups, ring), name='moe_l...  142 us

profile of v3, /device:TPU:33, one launch (start us, length us, event | category | flops | bytes accessed | tf_op | source)
XLA Modules:
  0.0 146.1 jit_solution(13164207187098953645)
XLA Ops:
  0.6 142.2 %moe_layer.1 = f32[2,128,512]{2,1,0:T(8,128)} custom-call(bf16[128,512]{1,0:T(8,128)(2,1)} %tok_ref.1, s32[8,128]{1,0:T(8,128)} %bitcast.6, f32[8,128]{1,0:T(8,128)} %bitcast.7, bf16[2,192,4096]{2,1,0:T(8,128)(2,1)} %gate_hbm.1, bf16[2,192,4096]{2,1,0:T(8,128)(2,1)} %up_hbm.1, bf16[2,1536,512]{2,1,0:T(8,128)(2,1)} %down_hbm.1), custom_call_target="tpu_custom_call" | custom-call | tf_op jit(solution)/shard_map/moe_layer/pallas_call | solution.py:848
  142.8 1.6 %fusion = bf16[128,512]{1,0:T(8,128)(2,1)} fusion(f32[2,128,512]{2,1,0:T(8,128)} %moe_layer.1), kind=kLoop, calls=%fused_computation.2 | loop fusion | bytes 262144 | tf_op jit(solution)/shard_map/convert_element_type | solution.py:927
  144.4 1.7 %slice_bitcast_fusion = f32[128,512]{1,0:T(8,128)} fusion(f32[2,128,512]{2,1,0:T(8,128)} %moe_layer.1), kind=kLoop, calls=%fused_computation.1 | loop fusion | bytes 524288 | tf_op jit(solution)/shard_map/squeeze | solution.py:927

commit v4 on v3

--- a/solution.py
+++ b/solution.py
@@ -653,10 +653,9 @@
         product = dot_nt(buf[...], weight_q[owner])
         acc_quant[at, :] = product if first else acc_quant[at, :] + product
 
-    def use_others(h):
+    def use_pair(h):
         left = lax.rem(x + ring - 1, ring)
         right = lax.rem(x + 1, ring)
-        across = lax.rem(x + 2, ring)
         await_step(0, rows, h, 1)
         if h == 0:
             await_step(3, rows, h, 1)
@@ -666,6 +665,9 @@
         level_rows(right, h, rows_q2)
         use_quant(left, h, False, rows_q)
         use_quant(right, h, False, rows_q2)
+
+    def use_across(h):
+        across = lax.rem(x + 2, ring)
         await_step(0, rows, h, 2)
         if h == 0:
             await_step(3, rows, h, 2)
@@ -739,7 +741,8 @@
     use_quant(x, 0, True, rows_q)
     relay(3, rows, 0)
     launch(0, rows, 1, (1,))
-    use_others(0)
+    use_pair(0)
+    use_across(0)
     activate(acc_float, hid_float, 0)
     launch(1, hid_float, 0, (0, 1))
     activate(acc_quant, hid_quant, 0)
@@ -753,13 +756,14 @@
     project(hid_float, down, outf_head, outf_rest, 0, False)
     send_back(1, 0, outf_head, outf_rest, backf_head, backf_rest)
     relay(2, hid_quant, 0)
+    far_arrive()
+    use_pair(1)
     await_step(2, hid_quant, 0, 1)
     await_step(2, hid_quant, 0, 2)
     levels(0)
     project(hid_level, down_q, outq_head, outq_rest, 0, True)
     send_back(2, 0, outq_head, outq_rest, backq_head, backq_rest)
-    far_arrive()
-    use_others(1)
+    use_across(1)
     activate(acc_float, hid_float, 1)
     launch(1, hid_float, 1, (0, 1))
     activate(acc_quant, hid_quant, 1)

time: 147 us -> 144 us (0.980)
  Pallas kernels: 142 us -> 139 us
    pallas_call x1, Pallas kernels: 142 us -> 139 us  [on_device(): pl.pallas_call(functools.partial(layer_kernel, groups, ring), name='moe_l...]
where the time goes in v4:
time: 144 us; the launch traced here: 143 us
  Pallas kernels  139 us (97%)
  local copies, waits for them, and re-layouts  3.29 us (2%)
    pallas_call x1, Pallas kernels, on_device(): pl.pallas_call(functools.partial(layer_kernel, groups, ring), name='moe_l...  139 us

profile of v4, /device:TPU:33, one launch (start us, length us, event | category | flops | bytes accessed | tf_op | source)
XLA Modules:
  0.0 142.5 jit_solution(2825698655289667603)
XLA Ops:
  0.6 138.6 %moe_layer.1 = f32[2,128,512]{2,1,0:T(8,128)} custom-call(bf16[128,512]{1,0:T(8,128)(2,1)} %tok_ref.1, s32[8,128]{1,0:T(8,128)} %bitcast.6, f32[8,128]{1,0:T(8,128)} %bitcast.7, bf16[2,192,4096]{2,1,0:T(8,128)(2,1)} %gate_hbm.1, bf16[2,192,4096]{2,1,0:T(8,128)(2,1)} %up_hbm.1, bf16[2,1536,512]{2,1,0:T(8,128)(2,1)} %down_hbm.1), custom_call_target="tpu_custom_call" | custom-call | tf_op jit(solution)/shard_map/moe_layer/pallas_call | solution.py:852
  139.2 1.6 %fusion = bf16[128,512]{1,0:T(8,128)(2,1)} fusion(f32[2,128,512]{2,1,0:T(8,128)} %moe_layer.1), kind=kLoop, calls=%fused_computation.2 | loop fusion | bytes 262144 | tf_op jit(solution)/shard_map/convert_element_type | solution.py:931
  140.8 1.7 %slice_bitcast_fusion = f32[128,512]{1,0:T(8,128)} fusion(f32[2,128,512]{2,1,0:T(8,128)} %moe_layer.1), kind=kLoop, calls=%fused_computation.1 | loop fusion | bytes 524288 | tf_op jit(solution)/shard_map/squeeze | solution.py:931

commit v5 on v4

--- a/solution.py
+++ b/solution.py
@@ -760,15 +760,15 @@
     use_pair(1)
     await_step(2, hid_quant, 0, 1)
     await_step(2, hid_quant, 0, 2)
-    levels(0)
-    project(hid_level, down_q, outq_head, outq_rest, 0, True)
-    send_back(2, 0, outq_head, outq_rest, backq_head, backq_rest)
     use_across(1)
     activate(acc_float, hid_float, 1)
     launch(1, hid_float, 1, (0, 1))
     activate(acc_quant, hid_quant, 1)
+    levels(0)
     relay(1, hid_float, 1)
     launch(2, hid_quant, 1, (0, 1))
+    project(hid_level, down_q, outq_head, outq_rest, 0, True)
+    send_back(2, 0, outq_head, outq_rest, backq_head, backq_rest)
     await_step(1, hid_float, 1, 1)
     await_step(1, hid_float, 1, 2)
     project(hid_float, down, outf_head, outf_rest, 1, False)

time: 144 us -> 146 us (1.014)
  Pallas kernels: 139 us -> 141 us
    pallas_call x1, Pallas kernels: 139 us -> 141 us  [on_device(): pl.pallas_call(functools.partial(layer_kernel, groups, ring), name='moe_l...]
where the time goes in v5:
time: 146 us; the launch traced here: 145 us
  Pallas kernels  141 us (97%)
  local copies, waits for them, and re-layouts  3.29 us (2%)
    pallas_call x1, Pallas kernels, on_device(): pl.pallas_call(functools.partial(layer_kernel, groups, ring), name='moe_l...  141 us

profile of v5, /device:TPU:33, one launch (start us, length us, event | category | flops | bytes accessed | tf_op | source)
XLA Modules:
  0.0 145.3 jit_solution(8570306365574101227)
XLA Ops:
  0.6 141.3 %moe_layer.1 = f32[2,128,512]{2,1,0:T(8,128)} custom-call(bf16[128,512]{1,0:T(8,128)(2,1)} %tok_ref.1, s32[8,128]{1,0:T(8,128)} %bitcast.6, f32[8,128]{1,0:T(8,128)} %bitcast.7, bf16[2,192,4096]{2,1,0:T(8,128)(2,1)} %gate_hbm.1, bf16[2,192,4096]{2,1,0:T(8,128)(2,1)} %up_hbm.1, bf16[2,1536,512]{2,1,0:T(8,128)(2,1)} %down_hbm.1), custom_call_target="tpu_custom_call" | custom-call | tf_op jit(solution)/shard_map/moe_layer/pallas_call | solution.py:852
  142.0 1.6 %fusion = bf16[128,512]{1,0:T(8,128)(2,1)} fusion(f32[2,128,512]{2,1,0:T(8,128)} %moe_layer.1), kind=kLoop, calls=%fused_computation.2 | loop fusion | bytes 262144 | tf_op jit(solution)/shard_map/convert_element_type | solution.py:931
  143.6 1.7 %slice_bitcast_fusion = f32[128,512]{1,0:T(8,128)} fusion(f32[2,128,512]{2,1,0:T(8,128)} %moe_layer.1), kind=kLoop, calls=%fused_computation.1 | loop fusion | bytes 524288 | tf_op jit(solution)/shard_map/squeeze | solution.py:931
